TPU v7x, 1024 devices: a whole 8x8x8 slice. The times are simulated.
1024 devices in a mesh: tile: 64 (over z, y), slab: 16 (over x, core).
Axes of the slice: x: 8, y: 8, z: 8, core: 2. Of those that a mesh axis runs over, the one named last changes fastest.
Arguments:
- amplitudes: float32 [64, 768, 96], P('tile'), may hold values from -6 to 6
- cholesky: float32 [512, 768, 96], P('slab'), may hold values from -0.12873545 to 0.12873545
- pair_occ: int32 [64, 2], replicated, may hold values from 0 to 63
- hole_integrals: float32 [64, 64], replicated, may hold values from -2 to 2
- other_terms: float32 [64, 768, 96], P('tile', 'slab'), may hold values from -6 to 6
- occ_energy: float32 [64], replicated, may hold values from -2 to -0.4
- vir_energy: float32 [768], replicated, may hold values from 0.2 to 3
Outputs:
- amp_new: float32 [64, 768, 96], P('tile', 'slab')
All inputs are finite; a program needn't handle non-finite values.
Results may differ from a plain program's by a relative error of at most 0.0001.
Values sent between devices are 32-bit elements; how exact they have to be, the bound alone decides.
No kernel may reach another device: no remote copies, remote signals or barrier semaphores. Data moves between devices by JAX's collectives and lax.ppermute only.
A program may use at most 32 MiB of HBM per device.

v0:
```python
import jax
import jax.numpy as jnp
from jax import lax
from jax.sharding import PartitionSpec as P


def local(amplitudes, cholesky, pair_occ, hole_integrals, other_terms, occ_energy, vir_energy):
    pair_dev, rows_all, width = amplitudes.shape
    occ_block = occ_energy.shape[0] // 8
    first = lax.axis_index("tile") * pair_dev
    irreps = jnp.bitwise_xor(pair_occ[:, 0] // occ_block, pair_occ[:, 1] // occ_block)
    mine = lax.dynamic_slice_in_dim(irreps, first, pair_dev, 0)
    my_pairs = lax.dynamic_slice_in_dim(pair_occ, first, pair_dev, 0)
    blocks = jnp.arange(8, dtype=jnp.int32)
    partner = jnp.bitwise_xor(blocks[None, :], mine[:, None])
    tiles = amplitudes.reshape(pair_dev, 8, width, width)

    def ladder_step(total, vectors):
        left = vectors.reshape(8, width, width)
        right = jnp.take(left, partner, axis=0)
        middle = jnp.einsum("pkcd,pkbd->pkcb", tiles, right, precision=lax.Precision.HIGHEST)
        return (
            total + jnp.einsum("kac,pkcb->pkab", left, middle, precision=lax.Precision.HIGHEST),
            None,
        )

    ladder, _ = lax.scan(ladder_step, jnp.zeros((pair_dev, 8, width, width), jnp.float32), cholesky)
    ladder = ladder.reshape(pair_dev, rows_all, width)
    masked = hole_integrals * (irreps[:, None] == irreps[None, :]).astype(jnp.float32)
    slab_count = lax.axis_size("slab")
    slab_pos = lax.axis_index("slab")
    rows_dev = rows_all // slab_count
    row_start = slab_pos * rows_dev
    columns = lax.all_to_all(amplitudes, "tile", split_axis=1, concat_axis=0, tiled=True)
    flat = columns.reshape(columns.shape[0], -1)
    product = jnp.dot(masked, flat, precision=lax.Precision.HIGHEST).reshape(columns.shape)
    hole_all = lax.all_to_all(product, "tile", split_axis=0, concat_axis=1, tiled=True)
    hole_rows = lax.dynamic_slice_in_dim(hole_all, row_start, rows_dev, 1)
    totals = lax.psum(ladder, "slab")
    summed = lax.dynamic_slice_in_dim(totals, row_start, rows_dev, 1)
    residual = other_terms + summed + hole_rows
    pair_energy = jnp.take(occ_energy, my_pairs[:, 0]) + jnp.take(occ_energy, my_pairs[:, 1])
    partner_energy = jnp.take(vir_energy.reshape(8, width), partner, axis=0)
    row_block = (row_start + jnp.arange(rows_dev, dtype=jnp.int32)) // width
    column_energy = jnp.take(partner_energy, row_block, axis=1)
    row_energy = lax.dynamic_slice_in_dim(vir_energy, row_start, rows_dev, 0)
    denominator = pair_energy[:, None, None] - row_energy[None, :, None] - column_energy
    return residual / denominator


def solution(mesh):
    placed = (
        P("tile", None, None),
        P("slab", None, None),
        P(),
        P(),
        P("tile", "slab", None),
        P(),
        P(),
    )
    return jax.shard_map(
        local, mesh=mesh, in_specs=placed, out_specs=P("tile", "slab", None), check_vma=False
    )
```

profile of v0, /device:TPU:1, one launch (start us, length us, event | category | flops | bytes accessed | tf_op | source)
XLA Modules:
  0.0 310.3 jit_solution(7384351885643176003)
XLA Ops:
  7.3 1.1 copy.17
  9.1 158.8 %while.13 = (s32[]{:T(128)}, f32[1,8,96,96]{2,3,1,0:T(8,128)S(1)}, f32[32,768,96]{1,2,0:T(8,128)}, f32[1,8,96,96]{3,2,1,0:T(8,128)S(1)}, s32[]{:T(128)}, /*index=5*/s32[]{:T(128)}, s32[]{:T(128)}) while((s32[]{:T(128)}, f32[1,8,96,96]{2,3,1,0:T(8,128)S(1)}, f32[32,768,96]{1,2,0:T(8,128)}, f32[1,8,96,96]{3,2,1,0:T(8,128)S(1)}, ...), condition=%wide.region_1.2_spmd.clone, body=%wide.region_0.1_spmd.clone.sunk | while | flops 170091616 | bytes 3838163 | solution.py:27
  9.1 1.0 constant_dynamic-slice_fusion.3
  14.1 1.0 constant_dynamic-slice_fusion.3
  19.0 1.0 constant_dynamic-slice_fusion.3
  24.0 1.0 constant_dynamic-slice_fusion.3
  28.9 1.0 constant_dynamic-slice_fusion.3
  33.9 1.0 constant_dynamic-slice_fusion.3
  38.9 1.0 constant_dynamic-slice_fusion.3
  43.8 1.0 constant_dynamic-slice_fusion.3
  48.8 1.0 constant_dynamic-slice_fusion.3
  53.7 1.0 constant_dynamic-slice_fusion.3
  58.7 1.0 constant_dynamic-slice_fusion.3
  63.7 1.0 constant_dynamic-slice_fusion.3
  68.6 1.0 constant_dynamic-slice_fusion.3
  73.6 1.0 constant_dynamic-slice_fusion.3
  78.5 1.0 constant_dynamic-slice_fusion.3
  83.5 1.0 constant_dynamic-slice_fusion.3
  88.5 1.0 constant_dynamic-slice_fusion.3
  93.4 1.0 constant_dynamic-slice_fusion.3
  98.4 1.0 constant_dynamic-slice_fusion.3
  103.3 1.0 constant_dynamic-slice_fusion.3
  108.3 1.0 constant_dynamic-slice_fusion.3
  168.8 1.0 copy.20
  169.8 24.0 %all-to-all-start = ((f32[1,768,96]{2,0,1:T(1,128)}), f32[1,768,96]{2,0,1:T(1,128)S(1)}, u32[]{:S(2)}, u32[]{:S(2)}) async-start(f32[1,768,96]{2,0,1:T(1,128)} %copy.20), calls=%async_computation | async-start | bytes 786432 | tf_op jit(solution)/shard_map/all_to_all | solution.py:34
  194.5 14.2 %all-to-all-done = f32[1,768,96]{2,0,1:T(1,128)S(1)} async-done(((f32[1,768,96]{2,0,1:T(1,128)}), f32[1,768,96]{2,0,1:T(1,128)S(1)}, u32[]{:S(2)}, u32[]{:S(2)}) %all-to-all-start) | async-done | bytes 294944 | tf_op jit(solution)/shard_map/all_to_all | solution.py:34
  209.3 1.6 reduce.3
  211.9 1.0 copy.22
  213.0 6.1 %all-to-all-start.1 = ((f32[64,12,96]{2,1,0:T(8,128)}), f32[64,12,96]{2,1,0:T(8,128)S(1)}, u32[]{:S(2)}, u32[]{:S(2)}) async-start(f32[64,12,96]{2,1,0:T(8,128)} %copy.22), calls=%async_computation.1 | async-start | bytes 1048576 | tf_op jit(solution)/shard_map/all_to_all | solution.py:37
  227.4 7.5 %all-to-all-done.1 = f32[64,12,96]{2,1,0:T(8,128)S(1)} async-done(((f32[64,12,96]{2,1,0:T(8,128)}), f32[64,12,96]{2,1,0:T(8,128)S(1)}, u32[]{:S(2)}, u32[]{:S(2)}) %all-to-all-start.1) | async-done | bytes 294944 | tf_op jit(solution)/shard_map/all_to_all | solution.py:37
  234.9 67.1 %all-reduce.2.cloned.1.call-done = f32[1,768,96]{2,1,0:T(8,128)} async-done(((f32[1,768,96]{2,1,0:T(8,128)}), f32[1,768,96]{2,1,0:T(8,128)}) %all-reduce.2.cloned.1.call-update) | async-done | bytes 294928 | tf_op jit(solution)/shard_map/psum | solution.py:39
  302.0 1.4 fusion.16
  (273 shorter events, 143.8 us)
Async XLA Ops:
  6.5 295.4 %all-reduce.2.cloned.1.call-start = ((), (), s32[]{:S(2)}) async-start(), calls=%async_computation.2 | async-start | bytes 786432 | tf_op jit(solution)/shard_map/psum | solution.py:39
  9.0 159.8 %copy-start = (f32[1,768,96]{1,2,0:T(8,128)S(1)}, f32[1,768,96]{1,2,0:T(8,128)}, u32[]{:S(2)}) copy-start(f32[1,768,96]{1,2,0:T(8,128)} %param.9) | copy-start | bytes 884740
  9.0 185.4 %copy-start.5 = (s32[64,2]{0,1:T(2,128)S(1)}, s32[64,2]{0,1:T(2,128)}, u32[]{:S(2)}) copy-start(s32[64,2]{0,1:T(2,128)} %param.11) | copy-start | bytes 1540
  9.0 202.3 %copy-start.1 = (f32[64,64]{1,0:T(8,128)S(1)}, f32[64,64]{1,0:T(8,128)}, u32[]{:S(2)}) copy-start(f32[64,64]{1,0:T(8,128)} %param.12) | copy-start | bytes 49156
  9.0 210.7 %copy-start.3 = (f32[768]{0:T(1024)S(1)}, f32[768]{0:T(1024)}, u32[]{:S(2)}) copy-start(f32[768]{0:T(1024)} %param.15) | copy-start | bytes 9220
  9.0 215.8 %copy-start.4 = (f32[64]{0:T(128)S(1)}, f32[64]{0:T(128)}, u32[]{:S(2)}) copy-start(f32[64]{0:T(128)} %param.14) | copy-start | bytes 772
  9.0 292.9 %copy-start.2 = (f32[1,48,96]{2,1,0:T(8,128)S(1)}, f32[1,48,96]{2,1,0:T(8,128)}, u32[]{:S(2)}) copy-start(f32[1,48,96]{2,1,0:T(8,128)} %param.13) | copy-start | bytes 55300
  169.8 39.0 %all-to-all-start = ((f32[1,768,96]{2,0,1:T(1,128)}), f32[1,768,96]{2,0,1:T(1,128)S(1)}, u32[]{:S(2)}, u32[]{:S(2)}) async-start(f32[1,768,96]{2,0,1:T(1,128)} %copy.20), calls=%async_computation | async-start | bytes 786432 | tf_op jit(solution)/shard_map/all_to_all | solution.py:34
  213.0 21.9 %all-to-all-start.1 = ((f32[64,12,96]{2,1,0:T(8,128)}), f32[64,12,96]{2,1,0:T(8,128)S(1)}, u32[]{:S(2)}, u32[]{:S(2)}) async-start(f32[64,12,96]{2,1,0:T(8,128)} %copy.22), calls=%async_computation.1 | async-start | bytes 1048576 | tf_op jit(solution)/shard_map/all_to_all | solution.py:37
Sparse Core Ops, SparseCore 0:
  168.9 133.0 all-reduce.1
where the time goes:
time: 312 us; the launch traced here: 310 us
  waiting for transfers between devices  88.7 us (28%)
  local copies, waits for them, and re-layouts  63.4 us (20%)
  matrix products  59.8 us (19%)
  other arithmetic  47.5 us (15%)
  starting transfers between devices  30 us (10%)
  between operations  18.6 us (6%)
    psum x1, waiting for transfers between devices, local(): totals = lax.psum(ladder, 'slab')  67.1 us
    dynamic_slice x64, local copies, waits for them, and re-layouts, local(): lax.scan(ladder_step, jnp.zeros((pair_dev, 8, width, width), jnp.float32)...  36.8 us
    dot_general x32, matrix products, ladder_step(): jnp.einsum('pkcd,pkbd->pkcb', tiles, right, precision=lax.Precision.HIGHEST)  30.7 us
    dot_general x32, matrix products, ladder_step(): jnp.einsum('kac,pkcb->pkab', left, middle, precision=lax.Precision.HIGHEST)  28.5 us
    all_to_all x1, starting transfers between devices, local(): lax.all_to_all(amplitudes, 'tile', split_axis=1, concat_axis=0, tiled=True)  24 us
    select_n x32, other arithmetic, ladder_step(): right = jnp.take(left, partner, axis=0)  21 us
    and x32, other arithmetic, ladder_step(): right = jnp.take(left, partner, axis=0)  21 us
    gather x32, local copies, waits for them, and re-layouts, ladder_step(): right = jnp.take(left, partner, axis=0)  18.4 us
  transfers between devices with their start and end apart: 3, of which 3 were waited for; matrix products, arithmetic and copies ran while one was open for 3% of the time, Pallas kernels for 0%

commit v1 on v0

v1 whole, which is shorter than its diff:
```python
import functools

import jax
import jax.numpy as jnp
from jax import lax
from jax.experimental import pallas as pl
from jax.experimental.pallas import tpu as pltpu
from jax.sharding import PartitionSpec as P

LANES = 128
Y = 8


def split(x):
    high = x.astype(jnp.bfloat16)
    return high, (x - high.astype(jnp.float32)).astype(jnp.bfloat16)


def irrep_of(pair_ref, pair, occ_block):
    return lax.bitwise_xor(
        lax.div(pair_ref[pair, 0], occ_block), lax.div(pair_ref[pair, 1], occ_block)
    )


def head_kernel(amp_t_ref, amp_ref, mine_ref):
    width = amp_t_ref.shape[0]
    rows_dev = mine_ref.shape[1]
    padded = jnp.concatenate(
        [amp_t_ref[...], jnp.zeros((LANES - width, amp_t_ref.shape[1]), jnp.float32)], axis=0
    )
    amp_ref[...] = jnp.transpose(padded)[:, :width]
    start = pl.multiple_of(lax.axis_index("slab") * rows_dev, 8)
    rows = amp_ref[pl.ds(start, rows_dev), :]
    for copy in range(mine_ref.shape[0]):
        mine_ref[copy] = rows


def ladder_kernel(occ_block, pair_ref, amp_ref, vec_ref, out_ref, weight, left, right, total):
    step = pl.program_id(0)
    count, width, rows_all = vec_ref.shape
    irrep = irrep_of(pair_ref, lax.axis_index("tile"), occ_block)

    @pl.when(step == 0)
    def _():
        weight[...] = jnp.zeros_like(weight)
        right[...] = jnp.zeros_like(right)
        total[...] = jnp.zeros_like(total)
        for block in range(8):
            high, low = split(amp_ref[block * width : (block + 1) * width, :])
            for row in (0, LANES):
                weight[block, row : row + width, :width] = high
                weight[block, row : row + width, LANES : LANES + width] = low

    def prepare(q):
        x = vec_ref[q]
        padded = jnp.concatenate([x, jnp.zeros((LANES - width, rows_all), jnp.float32)], axis=0)
        high, low = split(jnp.transpose(padded))
        left[q, :, :LANES] = high
        left[q, :, LANES:] = low
        high, low = split(x)
        for block in range(8):
            columns = slice(block * width, (block + 1) * width)
            right[block, q * LANES : q * LANES + width, :width] = high[:, columns]
            right[block, q * LANES : q * LANES + width, LANES : LANES + width] = low[:, columns]

    for q in range(count):
        prepare(q)

    for block in range(8):
        rows = left[:, block * width : (block + 1) * width, :].reshape(count * width, 2 * LANES)
        both = jnp.dot(rows, weight[block], preferred_element_type=jnp.float32)
        high, low = split(both[:, :LANES] + both[:, LANES:])
        middle = jnp.concatenate(
            [
                jnp.concatenate([part[q * width : (q + 1) * width] for q in range(count)], axis=1)
                for part in (high, low)
            ],
            axis=0,
        )
        total[block] += jnp.dot(
            middle, right[lax.bitwise_xor(block, irrep)], preferred_element_type=jnp.float32
        )

    @pl.when(step == pl.num_programs(0) - 1)
    def _():
        half = width // 2
        for block in range(8):
            value = (
                total[block, :width, :width]
                + total[block, :width, LANES : LANES + width]
                + total[block, width:, :width]
                + total[block, width:, LANES : LANES + width]
            )
            out_ref[2 * block] = value[:half]
            out_ref[2 * block + 1] = value[half:]


def hole_kernel(occ_block, pair_ref, integral_ref, rows_ref, out_ref):
    me = lax.axis_index("tile")
    my_z, my_y = lax.div(me, Y), lax.rem(me, Y)
    tiles = [rows_ref[y] for y in range(Y)]
    sources = [irrep_of(pair_ref, my_z * Y + y, occ_block) for y in range(Y)]
    for z in range(out_ref.shape[0]):
        target = z * Y + my_y
        irrep = irrep_of(pair_ref, target, occ_block)
        value = None
        for y in range(Y):
            factor = jnp.where(irrep == sources[y], integral_ref[target, my_z * Y + y], 0.0)
            term = factor * tiles[y]
            value = term if value is None else value + term
        out_ref[z] = value


def final_kernel(occ_block, pair_ref, occ_ref, vir_ref, other_ref, ladder_ref, hole_ref, out_ref):
    pair = lax.axis_index("tile")
    slab = lax.axis_index("slab")
    rows, width = out_ref.shape
    irrep = irrep_of(pair_ref, pair, occ_block)
    block = lax.div(slab, 2)
    residual = other_ref[...]
    for piece in range(ladder_ref.shape[0]):
        residual = residual + ladder_ref[piece]
    for piece in range(hole_ref.shape[0]):
        residual = residual + hole_ref[piece]
    pair_energy = occ_ref[pair_ref[pair, 0]] + occ_ref[pair_ref[pair, 1]]
    column = vir_ref[pl.ds(lax.bitwise_xor(block, irrep), 1), :]
    own = vir_ref[pl.ds(block, 1), :]
    lane = lax.broadcasted_iota(jnp.int32, (rows, width), 1)
    row = lax.broadcasted_iota(jnp.int32, (rows, width), 0) + lax.rem(slab, 2) * rows
    row_energy = jnp.sum(jnp.where(lane == row, own, 0.0), axis=1, keepdims=True)
    out_ref[...] = residual / (pair_energy - row_energy - column)


def local(amplitudes, cholesky, pair_occ, hole_integrals, other_terms, occ_energy, vir_energy):
    _, rows_all, width = amplitudes.shape
    vectors = cholesky.shape[0]
    slabs = lax.axis_size("slab")
    tiles = lax.axis_size("tile")
    rows_dev = rows_all // slabs
    depth = tiles // Y
    occ_block = occ_energy.shape[0] // 8
    vmem = pl.BlockSpec(memory_space=pltpu.VMEM)
    smem = pl.BlockSpec(memory_space=pltpu.SMEM)
    groups_y = [[z * Y + y for y in range(Y)] for z in range(depth)]
    groups_z = [[z * Y + y for z in range(depth)] for y in range(Y)]

    amp, mine = pl.pallas_call(
        head_kernel,
        out_shape=(
            jax.ShapeDtypeStruct((rows_all, width), jnp.float32),
            jax.ShapeDtypeStruct((Y, rows_dev, width), jnp.float32),
        ),
        in_specs=[vmem],
        out_specs=(vmem, vmem),
        name="head",
    )(jnp.transpose(amplitudes[0]))
    gathered = lax.all_to_all(mine, "tile", 0, 0, axis_index_groups=groups_y, tiled=True)

    chunk = 8
    steps = vectors // chunk
    flops = 2 * vectors * 8 * width * 4 * LANES * LANES * 2
    ladder = pl.pallas_call(
        functools.partial(ladder_kernel, occ_block),
        grid=(steps,),
        out_shape=jax.ShapeDtypeStruct((slabs, rows_dev, width), jnp.float32),
        in_specs=[
            smem,
            pl.BlockSpec((rows_all, width), lambda i: (0, 0)),
            pl.BlockSpec((chunk, width, rows_all), lambda i: (i, 0, 0)),
        ],
        out_specs=pl.BlockSpec((slabs, rows_dev, width), lambda i: (0, 0, 0)),
        scratch_shapes=[
            pltpu.VMEM((8, 2 * LANES, 2 * LANES), jnp.bfloat16),
            pltpu.VMEM((chunk, rows_all, 2 * LANES), jnp.bfloat16),
            pltpu.VMEM((8, chunk * LANES, 2 * LANES), jnp.bfloat16),
            pltpu.VMEM((8, 2 * width, 2 * LANES), jnp.float32),
        ],
        compiler_params=pltpu.CompilerParams(vmem_limit_bytes=40 << 20),
        cost_estimate=pl.CostEstimate(flops=flops, bytes_accessed=cholesky.size * 4, transcendentals=0),
        name="ladder",
    )(pair_occ, amp, jnp.transpose(cholesky, (0, 2, 1)))
    partial = pl.pallas_call(
        functools.partial(hole_kernel, occ_block),
        out_shape=jax.ShapeDtypeStruct((depth, rows_dev, width), jnp.float32),
        in_specs=[smem, smem, vmem],
        out_specs=vmem,
        name="hole",
    )(pair_occ, hole_integrals, gathered)
    hole = lax.all_to_all(partial, "tile", 0, 0, axis_index_groups=groups_z, tiled=True)
    pieces = lax.all_to_all(ladder, "slab", 0, 0, tiled=True)
    out = pl.pallas_call(
        functools.partial(final_kernel, occ_block),
        out_shape=jax.ShapeDtypeStruct((rows_dev, width), jnp.float32),
        in_specs=[smem, smem, vmem, vmem, vmem, vmem],
        out_specs=vmem,
        name="final",
    )(pair_occ, occ_energy, vir_energy.reshape(8, width), other_terms[0], pieces, hole)
    return out[None]


def solution(mesh):
    placed = (
        P("tile", None, None),
        P("slab", None, None),
        P(),
        P(),
        P("tile", "slab", None),
        P(),
        P(),
    )
    return jax.shard_map(
        local, mesh=mesh, in_specs=placed, out_specs=P("tile", "slab", None), check_vma=False
    )
```

time: 312 us -> 87.5 us (0.28)
  waiting for transfers between devices: 88.7 us -> 21.1 us
  matrix products: 59.8 us -> 0 us
  local copies, waits for them, and re-layouts: 63.4 us -> 8.89 us
  other arithmetic: 47.5 us -> 0 us
  Pallas kernels: 0 us -> 22.4 us
  between operations: 18.6 us -> 0.02 us
  starting transfers between devices: 30 us -> 34.4 us
    psum x1 -> x0, waiting for transfers between devices: 67.1 us -> none  [local(): totals = lax.psum(ladder, 'slab')]
    dot_general x65 -> x0, matrix products: 59.8 us -> none  [the longest x32 30.7 us: ladder_step(): jnp.einsum('pkcd,pkbd->pkcb', tiles, right, precision=lax.Precision.HIGHEST)]
    dynamic_slice x66 -> x0, local copies, waits for them, and re-layouts: 37.5 us -> none  [the longest x64 36.8 us: local(): lax.scan(ladder_step, jnp.zeros((pair_dev, 8, width, width), jnp.float32)...]
    pallas_call x0 -> x4, Pallas kernels: none -> 22.4 us  [the longest x1 15.7 us: local(): pl.pallas_call(functools.partial(ladder_kernel, occ_block), grid=(steps,)...]
    select_n x35 -> x0, other arithmetic: 21.7 us -> none  [the longest x32 21 us: ladder_step(): right = jnp.take(left, partner, axis=0)]
    and x34 -> x0, other arithmetic: 21.7 us -> none  [the longest x32 21 us: ladder_step(): right = jnp.take(left, partner, axis=0)]
    gather x35 -> x0, local copies, waits for them, and re-layouts: 20.2 us -> none  [the longest x32 18.4 us: ladder_step(): right = jnp.take(left, partner, axis=0)]
    unnamed x14 -> x15, local copies, waits for them, and re-layouts: 2.15 us -> 8.23 us
  transfers between devices with their start and end apart: 3 -> 3, of which waited for: 3 -> 2; matrix products, arithmetic and copies ran while one was open for 3% -> 2% of each run, Pallas kernels for 0% -> 18%
where the time goes in v1:
time: 87.5 us; the launch traced here: 86.8 us
  starting transfers between devices  34.4 us (39%)
  Pallas kernels  22.4 us (26%)
  waiting for transfers between devices  21.1 us (24%)
  local copies, waits for them, and re-layouts  8.89 us (10%)
    all_to_all x1, starting transfers between devices, local(): lax.all_to_all(partial, 'tile', 0, 0, axis_index_groups=groups_z, tiled=T...  16.6 us
    pallas_call x1, Pallas kernels, local(): pl.pallas_call(functools.partial(ladder_kernel, occ_block), grid=(steps,)...  15.7 us
    all_to_all x1, waiting for transfers between devices, local(): pieces = lax.all_to_all(ladder, 'slab', 0, 0, tiled=True)  13.9 us
    all_to_all x1, starting transfers between devices, local(): pieces = lax.all_to_all(ladder, 'slab', 0, 0, tiled=True)  9.66 us
    unnamed x15, local copies, waits for them, and re-layouts  8.23 us
    all_to_all x1, starting transfers between devices, local(): lax.all_to_all(mine, 'tile', 0, 0, axis_index_groups=groups_y, tiled=True)  8.11 us
    all_to_all x1, waiting for transfers between devices, local(): lax.all_to_all(mine, 'tile', 0, 0, axis_index_groups=groups_y, tiled=True)  7.26 us
    pallas_call x1, Pallas kernels, local(): pl.pallas_call(functools.partial(hole_kernel, occ_block), out_shape=jax.S...  2.63 us
  transfers between devices with their start and end apart: 3, of which 2 were waited for; matrix products, arithmetic and copies ran while one was open for 2% of the time, Pallas kernels for 18%

profile of v1, /device:TPU:1, one launch (start us, length us, event | category | flops | bytes accessed | tf_op | source)
XLA Modules:
  0.0 86.8 jit_solution(14968469455448583529)
XLA Ops:
  0.0 1.9 %head.1 = (f32[768,96]{1,0:T(8,128)}, f32[8,48,96]{2,1,0:T(8,128)}) custom-call(f32[96,768]{1,0:T(8,128)} %bitcast.7), custom_call_target="tpu_custom_call" | custom-call | tf_op jit(solution)/shard_map/head/pallas_call | solution.py:147
  1.9 8.1 %all-to-all-start.1 = ((f32[8,48,96]{2,1,0:T(8,128)}), f32[8,48,96]{2,1,0:T(8,128)S(1)}, u32[]{:S(2)}, u32[]{:S(2)}) async-start(f32[8,48,96]{2,1,0:T(8,128)} %get-tuple-element.8), calls=%async_computation.1 | async-start | bytes 393216 | tf_op jit(solution)/shard_map/all_to_all | solution.py:157
  10.1 1.4 %copy.10.pair_ref = s32[64,2]{1,0:T(8,128)} copy(s32[64,2]{0,1:T(2,128)} %param.9) | data formatting | bytes 1024 | tf_op args[2]
  11.4 7.3 %all-to-all-done.1.rows_ref = f32[8,48,96]{2,1,0:T(8,128)S(1)} async-done(((f32[8,48,96]{2,1,0:T(8,128)}), f32[8,48,96]{2,1,0:T(8,128)S(1)}, u32[]{:S(2)}, u32[]{:S(2)}) %all-to-all-start.1) | async-done | bytes 147488 | tf_op jit(solution)/shard_map/all_to_all | solution.py:157
  18.7 0.0 copy-start.4
  18.7 0.7 copy-done.4
  19.4 2.6 %hole.1 = f32[8,48,96]{2,1,0:T(8,128)} custom-call(s32[64,2]{1,0:T(8,128)} %copy.10.pair_ref, f32[64,64]{1,0:T(8,128)} %integral_ref.1, f32[8,48,96]{2,1,0:T(8,128)} %copy-done.4), custom_call_target="tpu_custom_call" | custom-call | tf_op jit(solution)/shard_map/hole/pallas_call | solution.py:182
  22.0 16.6 %all-to-all-start.2 = ((f32[8,48,96]{2,1,0:T(8,128)}), f32[8,48,96]{2,1,0:T(8,128)S(1)}, u32[]{:S(2)}, u32[]{:S(2)}) async-start(f32[8,48,96]{2,1,0:T(8,128)} %hole.1), calls=%async_computation.2 | async-start | bytes 393216 | tf_op jit(solution)/shard_map/all_to_all | solution.py:189
  38.6 0.0 copy-start
  38.6 0.8 copy-done
  39.4 0.0 copy-start.1
  39.4 3.7 %copy-done.1 = f32[32,768,96]{1,2,0:T(8,128)S(1)} copy-done((f32[32,768,96]{1,2,0:T(8,128)S(1)}, f32[32,768,96]{1,2,0:T(8,128)}, u32[]{:S(2)}) %copy-start.1) | copy-done | bytes 9437208
  43.0 0.0 copy-start.2
  43.0 1.0 %copy-done.2 = f32[768,96]{1,0:T(8,128)S(1)} copy-done((f32[768,96]{1,0:T(8,128)S(1)}, f32[768,96]{1,0:T(8,128)}, u32[]{:S(2)}) %copy-start.2) | copy-done | bytes 294936
  44.0 0.0 copy-start.6
  44.0 15.7 %ladder.1 = f32[16,48,96]{2,1,0:T(8,128)} custom-call(s32[64,2]{1,0:T(8,128)S(1)} %copy-done, f32[768,96]{1,0:T(8,128)S(1)} %copy-done.2, f32[32,96,768]{2,1,0:T(8,128)S(1)} %bitcast.6), custom_call_target="tpu_custom_call" | custom-call | flops 6442450944 | bytes 9437184 | tf_op jit(solution)/shard_map/ladder/pallas_call | solution.py:162
  59.8 0.0 all-to-all-done.2.hole_ref
  59.8 0.0 copy-start.5
  59.8 9.7 %all-to-all-start = ((f32[16,48,96]{2,1,0:T(8,128)}), f32[16,48,96]{2,1,0:T(8,128)S(1)}, u32[]{:S(2)}, u32[]{:S(2)}) async-start(f32[16,48,96]{2,1,0:T(8,128)} %ladder.1), calls=%async_computation | async-start | bytes 786432 | tf_op jit(solution)/shard_map/all_to_all | solution.py:190
  69.4 0.0 copy-done.6
  69.4 0.7 reshape.3.vir_ref
  70.1 13.9 %all-to-all-done.ladder_ref = f32[16,48,96]{2,1,0:T(8,128)S(1)} async-done(((f32[16,48,96]{2,1,0:T(8,128)}), f32[16,48,96]{2,1,0:T(8,128)S(1)}, u32[]{:S(2)}, u32[]{:S(2)}) %all-to-all-start) | async-done | bytes 294944 | tf_op jit(solution)/shard_map/all_to_all | solution.py:190
  84.0 0.0 copy-start.3
  84.0 0.0 copy-done.5
  84.0 0.7 copy-done.3
  84.7 2.1 %final.1 = f32[48,96]{1,0:T(8,128)} custom-call(s32[64,2]{1,0:T(8,128)} %copy.10.pair_ref, f32[64]{0:T(128)} %occ_ref.1, f32[8,96]{1,0:T(8,128)} %reshape.3.vir_ref, f32[48,96]{1,0:T(8,128)} %bitcast.8, f32[16,48,96]{2,1,0:T(8,128)} %copy-done.3, f32[8,48,96]{2,1,0:T(8,128)} %copy-done.5), custom_call_target="tpu_custom_call" | custom-call | tf_op jit(solution)/shard_map/final/pallas_call | solution.py:191
Async XLA Ops:
  1.9 16.7 %all-to-all-start.1 = ((f32[8,48,96]{2,1,0:T(8,128)}), f32[8,48,96]{2,1,0:T(8,128)S(1)}, u32[]{:S(2)}, u32[]{:S(2)}) async-start(f32[8,48,96]{2,1,0:T(8,128)} %get-tuple-element.8), calls=%async_computation.1 | async-start | bytes 393216 | tf_op jit(solution)/shard_map/all_to_all | solution.py:157
  18.7 0.7 copy-start.4
  22.0 37.8 %all-to-all-start.2 = ((f32[8,48,96]{2,1,0:T(8,128)}), f32[8,48,96]{2,1,0:T(8,128)S(1)}, u32[]{:S(2)}, u32[]{:S(2)}) async-start(f32[8,48,96]{2,1,0:T(8,128)} %hole.1), calls=%async_computation.2 | async-start | bytes 393216 | tf_op jit(solution)/shard_map/all_to_all | solution.py:189
  38.6 0.8 copy-start
  39.4 3.7 %copy-start.1 = (f32[32,768,96]{1,2,0:T(8,128)S(1)}, f32[32,768,96]{1,2,0:T(8,128)}, u32[]{:S(2)}) copy-start(f32[32,768,96]{1,2,0:T(8,128)} %param.8) | copy-start | bytes 28311556
  43.0 1.0 %copy-start.2 = (f32[768,96]{1,0:T(8,128)S(1)}, f32[768,96]{1,0:T(8,128)}, u32[]{:S(2)}) copy-start(f32[768,96]{1,0:T(8,128)} %get-tuple-element.7.amp_ref) | copy-start | bytes 884740
  44.0 25.4 %copy-start.6 = (f32[768]{0:T(1024)S(1)}, f32[768]{0:T(1024)}, u32[]{:S(2)}) copy-start(f32[768]{0:T(1024)} %param.13) | copy-start | bytes 9220
  59.8 24.2 %copy-start.5 = (f32[8,48,96]{2,1,0:T(8,128)}, f32[8,48,96]{2,1,0:T(8,128)S(1)}, u32[]{:S(2)}) copy-start(f32[8,48,96]{2,1,0:T(8,128)S(1)} %all-to-all-done.2.hole_ref) | copy-start | bytes 442372
  59.8 24.2 %all-to-all-start = ((f32[16,48,96]{2,1,0:T(8,128)}), f32[16,48,96]{2,1,0:T(8,128)S(1)}, u32[]{:S(2)}, u32[]{:S(2)}) async-start(f32[16,48,96]{2,1,0:T(8,128)} %ladder.1), calls=%async_computation | async-start | bytes 786432 | tf_op jit(solution)/shard_map/all_to_all | solution.py:190
  84.0 0.7 copy-start.3

commit v2 on v1

v2 whole, which is shorter than its diff:
```python
import functools

import jax
import jax.numpy as jnp
from jax import lax
from jax.experimental import pallas as pl
from jax.experimental.pallas import tpu as pltpu
from jax.sharding import PartitionSpec as P

LANES = 128
Y = 8


def split(x):
    high = x.astype(jnp.bfloat16)
    return high, (x - high.astype(jnp.float32)).astype(jnp.bfloat16)


def irrep_of(pair_ref, pair, occ_block):
    return lax.bitwise_xor(
        lax.div(pair_ref[0, pair], occ_block), lax.div(pair_ref[1, pair], occ_block)
    )


def head_kernel(amp_t_ref, mine_ref, window, turned, sem):
    width, rows_all = amp_t_ref.shape
    copies, rows_dev, _ = mine_ref.shape
    span = window.shape[1]
    first = lax.axis_index("slab") * rows_dev
    base = jnp.minimum(lax.div(first, LANES) * LANES, rows_all - span)
    load = pltpu.make_async_copy(
        amp_t_ref.at[:, pl.ds(pl.multiple_of(base, LANES), span)], window, sem
    )
    load.start()
    load.wait()
    padded = jnp.concatenate(
        [window[...], jnp.zeros((LANES - width, span), jnp.float32)], axis=0
    )
    turned[...] = jnp.transpose(padded)
    rows = turned[pl.ds(pl.multiple_of(first - base, 8), rows_dev), :width]
    for copy in range(copies):
        mine_ref[copy] = rows


def ladder_kernel(
    occ_block, chunk, offset, pair_ref, amp_t_ref, after_ref, vec_hbm, *refs
):
    base_ref = refs[0] if offset else None
    out_ref, weight, left_even, left_odd, vectors, total, sem = refs[-7:]
    count, width, rows_all = vectors.shape
    chunks = count // chunk
    lefts = (left_even, left_odd)
    irrep = irrep_of(pair_ref, lax.axis_index("tile"), occ_block)
    loads = []
    bounds = list(range(chunk)) + [c * chunk for c in range(1, chunks + 1)]
    for index, (begin, end) in enumerate(zip(bounds[:-1], bounds[1:])):
        loads.append(
            pltpu.make_async_copy(
                vec_hbm.at[pl.ds(offset + begin, end - begin)],
                vectors.at[pl.ds(begin, end - begin)],
                sem.at[index],
            )
        )
        loads[-1].start()
    weight[...] = jnp.zeros_like(weight)
    amp = jnp.transpose(amp_t_ref[...])
    for block in range(8):
        high, low = split(amp[block * width : (block + 1) * width, :])
        for row in (0, LANES):
            weight[block, row : row + width, :width] = high
            weight[block, row : row + width, LANES : LANES + width] = low
    fill = jnp.zeros((LANES - width, rows_all), jnp.bfloat16)

    def prepare(c, q):
        for half, part in enumerate(split(vectors[c * chunk + q])):
            lefts[c % 2][q, :, half * LANES : (half + 1) * LANES] = jnp.transpose(
                jnp.concatenate([part, fill], axis=0)
            )

    def beside(parts):
        return jnp.concatenate(parts, axis=1)

    def first(c, block):
        rows = lefts[c % 2][:, block * width : (block + 1) * width, :]
        both = jnp.dot(
            rows.reshape(chunk * width, 2 * LANES),
            weight[block],
            preferred_element_type=jnp.float32,
        )
        parts = split(both[:, :LANES] + both[:, LANES:])
        return jnp.concatenate(
            [beside([x[q * width : (q + 1) * width] for q in range(chunk)]) for x in parts], axis=0
        )

    def second(c, block, middle):
        begin = pl.multiple_of(lax.bitwise_xor(block, irrep) * width, 16)
        rows = lefts[c % 2][:, pl.ds(begin, width), :]
        other = jnp.concatenate(
            [
                beside([rows[q, :, h * LANES : (h + 1) * LANES] for q in range(chunk)])
                for h in range(2)
            ],
            axis=0,
        )
        value = lax.dot_general(
            middle, other, (((1,), (1,)), ((), ())), preferred_element_type=jnp.float32
        )
        total[block] = value if c == 0 else total[block] + value

    for q in range(chunk):
        loads[q].wait()
        prepare(0, q)
    work = [(c, block) for c in range(chunks) for block in range(8)]
    middle = first(*work[0])
    for index, (c, block) in enumerate(work):
        if c + 1 < chunks:
            if block == 0:
                loads[chunk + c].wait()
            for q in range(block * chunk // 8, (block + 1) * chunk // 8):
                prepare(c + 1, q)
        following = first(*work[index + 1]) if index + 1 < len(work) else None
        second(c, block, middle)
        middle = following
    half = width // 2
    for block in range(8):
        value = (
            total[block, :width, :width]
            + total[block, :width, width:]
            + total[block, width:, :width]
            + total[block, width:, width:]
        )
        for part in range(2):
            rows = value[part * half : (part + 1) * half]
            if offset:
                rows = rows + base_ref[2 * block + part]
            out_ref[2 * block + part] = rows


def hole_kernel(occ_block, pair_ref, integral_ref, rows_ref, out_ref):
    me = lax.axis_index("tile")
    my_z, my_y = lax.div(me, Y), lax.rem(me, Y)
    tiles = [rows_ref[y] for y in range(Y)]
    sources = [irrep_of(pair_ref, my_z * Y + y, occ_block) for y in range(Y)]
    for z in range(out_ref.shape[0]):
        target = z * Y + my_y
        irrep = irrep_of(pair_ref, target, occ_block)
        value = None
        for y in range(Y):
            factor = jnp.where(irrep == sources[y], integral_ref[target, my_z * Y + y], 0.0)
            term = factor * tiles[y]
            value = term if value is None else value + term
        out_ref[z] = value


def final_kernel(occ_block, pair_ref, occ_ref, vir_ref, other_ref, ladder_ref, hole_ref, out_ref):
    pair = lax.axis_index("tile")
    slab = lax.axis_index("slab")
    rows, width = out_ref.shape
    irrep = irrep_of(pair_ref, pair, occ_block)
    block = lax.div(slab, 2)
    residual = other_ref[...]
    for piece in range(ladder_ref.shape[0]):
        residual = residual + ladder_ref[piece]
    for piece in range(hole_ref.shape[0]):
        residual = residual + hole_ref[piece]
    pair_energy = occ_ref[pair_ref[0, pair]] + occ_ref[pair_ref[1, pair]]
    column = vir_ref[pl.ds(lax.bitwise_xor(block, irrep), 1), :]
    own = vir_ref[pl.ds(block, 1), :]
    lane = lax.broadcasted_iota(jnp.int32, (rows, width), 1)
    row = lax.broadcasted_iota(jnp.int32, (rows, width), 0) + lax.rem(slab, 2) * rows
    row_energy = jnp.sum(jnp.where(lane == row, own, 0.0), axis=1, keepdims=True)
    out_ref[...] = residual / (pair_energy - row_energy - column)


def local(amplitudes, cholesky, pair_occ, hole_integrals, other_terms, occ_energy, vir_energy):
    _, rows_all, width = amplitudes.shape
    vectors = cholesky.shape[0]
    slabs = lax.axis_size("slab")
    tiles = lax.axis_size("tile")
    rows_dev = rows_all // slabs
    depth = tiles // Y
    occ_block = occ_energy.shape[0] // 8
    vmem = pl.BlockSpec(memory_space=pltpu.VMEM)
    smem = pl.BlockSpec(memory_space=pltpu.SMEM)
    groups_y = [[z * Y + y for y in range(Y)] for z in range(depth)]
    groups_z = [[z * Y + y for z in range(depth)] for y in range(Y)]

    hbm = pl.BlockSpec(memory_space=pltpu.MemorySpace.HBM)
    small = pltpu.CompilerParams(vmem_limit_bytes=6 << 20)
    pairs = jnp.transpose(pair_occ)
    amp_t = jnp.transpose(amplitudes[0])
    vectors_t = jnp.transpose(cholesky, (0, 2, 1))

    mine = pl.pallas_call(
        head_kernel,
        out_shape=jax.ShapeDtypeStruct((Y, rows_dev, width), jnp.float32),
        in_specs=[hbm],
        out_specs=vmem,
        scratch_shapes=[
            pltpu.VMEM((width, 2 * LANES), jnp.float32),
            pltpu.VMEM((2 * LANES, LANES), jnp.float32),
            pltpu.SemaphoreType.DMA,
        ],
        compiler_params=pltpu.CompilerParams(vmem_limit_bytes=60 << 20),
        name="head",
    )(amp_t)
    gathered = lax.all_to_all(mine, "tile", 0, 0, axis_index_groups=groups_y, tiled=True)

    chunk = 8
    share = vectors // 2

    def ladder_part(offset, after, *base):
        flops = 2 * share * 8 * width * (2 * LANES) * (2 * LANES) * 2
        return pl.pallas_call(
            functools.partial(ladder_kernel, occ_block, chunk, offset),
            out_shape=jax.ShapeDtypeStruct((slabs, rows_dev, width), jnp.float32),
            in_specs=[smem, vmem, pl.BlockSpec(memory_space=pl.ANY), hbm] + [vmem] * len(base),
            out_specs=vmem,
            scratch_shapes=[
                pltpu.VMEM((8, 2 * LANES, 2 * LANES), jnp.bfloat16),
                pltpu.VMEM((chunk, rows_all, 2 * LANES), jnp.bfloat16),
                pltpu.VMEM((chunk, rows_all, 2 * LANES), jnp.bfloat16),
                pltpu.VMEM((share, width, rows_all), jnp.float32),
                pltpu.VMEM((8, 2 * width, 2 * width), jnp.float32),
                pltpu.SemaphoreType.DMA((chunk + share // chunk - 1,)),
            ],
            compiler_params=pltpu.CompilerParams(vmem_limit_bytes=58 << 20),
            cost_estimate=pl.CostEstimate(
                flops=flops, bytes_accessed=share * rows_all * width * 4, transcendentals=0
            ),
            name="ladder",
        )(pairs, amp_t, after, vectors_t, *base)

    ladder = ladder_part(0, mine)
    gathered, ladder = lax.optimization_barrier((gathered, ladder))
    partial = pl.pallas_call(
        functools.partial(hole_kernel, occ_block),
        out_shape=jax.ShapeDtypeStruct((depth, rows_dev, width), jnp.float32),
        in_specs=[smem, smem, vmem],
        out_specs=vmem,
        compiler_params=small,
        name="hole",
    )(pairs, hole_integrals, gathered)
    ladder = ladder_part(share, partial, ladder)
    pieces = lax.all_to_all(ladder, "slab", 0, 0, tiled=True)
    hole = lax.all_to_all(partial, "tile", 0, 0, axis_index_groups=groups_z, tiled=True)
    out = pl.pallas_call(
        functools.partial(final_kernel, occ_block),
        out_shape=jax.ShapeDtypeStruct((rows_dev, width), jnp.float32),
        in_specs=[smem, smem, vmem, vmem, vmem, vmem],
        out_specs=vmem,
        compiler_params=small,
        name="final",
    )(pairs, occ_energy, vir_energy.reshape(8, width), other_terms[0], pieces, hole)
    return out[None]


def solution(mesh):
    placed = (
        P("tile", None, None),
        P("slab", None, None),
        P(),
        P(),
        P("tile", "slab", None),
        P(),
        P(),
    )
    return jax.shard_map(
        local, mesh=mesh, in_specs=placed, out_specs=P("tile", "slab", None), check_vma=False
    )
```

time: 87.5 us -> 72.8 us (0.83)
  local copies, waits for them, and re-layouts: 8.89 us -> 0.1 us
  waiting for transfers between devices: 21.1 us -> 15.5 us
  Pallas kernels: 22.4 us -> 21.2 us
  starting transfers between devices: 34.4 us -> 35.4 us
    unnamed x15 -> x12, local copies, waits for them, and re-layouts: 8.23 us -> 0.03 us
    all_to_all x1, waiting for transfers between devices: 7.26 us -> 0.5 us  [local(): lax.all_to_all(mine, 'tile', 0, 0, axis_index_groups=groups_y, tiled=True)]
    all_to_all x1, starting transfers between devices: 9.66 us -> 10.7 us  [local(): pieces = lax.all_to_all(ladder, 'slab', 0, 0, tiled=True)]
    pallas_call x2 -> x3, Pallas kernels: 17.7 us -> 18 us  [the longest x2 16.3 us: ladder_part(): pl.pallas_call(functools.partial(ladder_kernel, occ_block, chunk, offset)...]
  transfers between devices with their start and end apart: 3 -> 3, of which waited for: 2 -> 3; matrix products, arithmetic and copies ran while one was open for 2% -> 0% of each run, Pallas kernels for 18% -> 23%
where the time goes in v2:
time: 72.8 us; the launch traced here: 72.3 us
  starting transfers between devices  35.4 us (49%)
  Pallas kernels  21.2 us (29%)
  waiting for transfers between devices  15.5 us (21%)
    all_to_all x1, starting transfers between devices, local(): lax.all_to_all(partial, 'tile', 0, 0, axis_index_groups=groups_z, tiled=T...  16.6 us
    pallas_call x2, Pallas kernels, ladder_part(): pl.pallas_call(functools.partial(ladder_kernel, occ_block, chunk, offset)...  16.3 us
    all_to_all x1, waiting for transfers between devices, local(): pieces = lax.all_to_all(ladder, 'slab', 0, 0, tiled=True)  14.5 us
    all_to_all x1, starting transfers between devices, local(): pieces = lax.all_to_all(ladder, 'slab', 0, 0, tiled=True)  10.7 us
    all_to_all x1, starting transfers between devices, local(): lax.all_to_all(mine, 'tile', 0, 0, axis_index_groups=groups_y, tiled=True)  8.12 us
    pallas_call x1, Pallas kernels, local(): pl.pallas_call(functools.partial(hole_kernel, occ_block), out_shape=jax.S...  2 us
    pallas_call x1, Pallas kernels, local(): pl.pallas_call(head_kernel, out_shape=jax.ShapeDtypeStruct((Y, rows_dev,...  1.7 us
  transfers between devices with their start and end apart: 3, of which 3 were waited for; matrix products, arithmetic and copies ran while one was open for 0% of the time, Pallas kernels for 23%

profile of v2, /device:TPU:1, one launch (start us, length us, event | category | flops | bytes accessed | tf_op | source)
XLA Modules:
  0.0 72.3 jit_solution(14791923498634657550)
XLA Ops:
  0.0 0.0 copy-start.2
  0.0 0.0 copy-start
  0.0 1.7 %head.1.after_ref = f32[8,48,96]{2,1,0:T(8,128)} custom-call(f32[96,768]{1,0:T(8,128)} %bitcast.12), custom_call_target="tpu_custom_call" | custom-call | tf_op jit(solution)/shard_map/head/pallas_call | solution.py:194
  1.7 8.1 %all-to-all-start = ((f32[8,48,96]{2,1,0:T(8,128)}), f32[8,48,96]{2,1,0:T(8,128)S(1)}, u32[]{:S(2)}, u32[]{:S(2)}) async-start(f32[8,48,96]{2,1,0:T(8,128)} %head.1.after_ref), calls=%async_computation | async-start | bytes 393216 | tf_op jit(solution)/shard_map/all_to_all | solution.py:207
  9.8 8.1 %ladder.2.refs_0_ = f32[16,48,96]{2,1,0:T(8,128)} custom-call(s32[2,64]{1,0:T(2,128)} %bitcast.8, f32[96,768]{1,0:T(8,128)} %bitcast.13, f32[8,48,96]{2,1,0:T(8,128)} %head.1.after_ref, f32[32,96,768]{2,1,0:T(8,128)} %bitcast.15), custom_call_target="tpu_custom_call" | custom-call | flops 3221225472 | bytes 4718592 | tf_op jit(solution)/shard_map/ladder/pallas_call | solution.py:214
  17.9 0.0 copy-start.5
  17.9 0.0 copy-start.1
  17.9 0.0 copy-start.3
  18.0 0.0 copy-start.4
  18.0 0.5 all-to-all-done.rows_ref
  18.5 0.0 copy-done.2
  18.5 0.0 copy-done
  18.5 2.0 %hole.1.after_ref = f32[8,48,96]{2,1,0:T(8,128)} custom-call(s32[2,64]{1,0:T(2,128)S(1)} %bitcast.10, f32[64,64]{1,0:T(8,128)S(1)} %copy-done, f32[8,48,96]{2,1,0:T(8,128)S(1)} %all-to-all-done.rows_ref), custom_call_target="tpu_custom_call" | custom-call | tf_op jit(solution)/shard_map/hole/pallas_call | solution.py:236
  20.5 16.6 %all-to-all-start.2 = ((f32[8,48,96]{2,1,0:T(8,128)}), f32[8,48,96]{2,1,0:T(8,128)S(1)}, u32[]{:S(2)}, u32[]{:S(2)}) async-start(f32[8,48,96]{2,1,0:T(8,128)} %hole.1.after_ref), calls=%async_computation.2 | async-start | bytes 393216 | tf_op jit(solution)/shard_map/all_to_all | solution.py:246
  37.1 8.2 %ladder.3 = f32[16,48,96]{2,1,0:T(8,128)} custom-call(s32[2,64]{1,0:T(2,128)} %bitcast.9, f32[96,768]{1,0:T(8,128)} %bitcast.14, f32[8,48,96]{2,1,0:T(8,128)} %hole.1.after_ref, f32[32,96,768]{2,1,0:T(8,128)} %bitcast.16, f32[16,48,96]{2,1,0:T(8,128)} %ladder.2.refs_0_), custom_call_target="tpu_custom_call" | custom-call | flops 3221225472 | bytes 4718592 | tf_op jit(solution)/shard_map/ladder/pallas_call | solution.py:214
  45.3 0.5 all-to-all-done.2.hole_ref
  45.8 10.7 %all-to-all-start.1 = ((f32[16,48,96]{2,1,0:T(8,128)}), f32[16,48,96]{2,1,0:T(8,128)S(1)}, u32[]{:S(2)}, u32[]{:S(2)}) async-start(f32[16,48,96]{2,1,0:T(8,128)} %ladder.3), calls=%async_computation.1 | async-start | bytes 786432 | tf_op jit(solution)/shard_map/all_to_all | solution.py:245
  56.5 0.0 copy-done.5
  56.5 0.1 reshape.3.vir_ref
  56.6 14.5 %all-to-all-done.1.ladder_ref = f32[16,48,96]{2,1,0:T(8,128)S(1)} async-done(((f32[16,48,96]{2,1,0:T(8,128)}), f32[16,48,96]{2,1,0:T(8,128)S(1)}, u32[]{:S(2)}, u32[]{:S(2)}) %all-to-all-start.1) | async-done | bytes 294944 | tf_op jit(solution)/shard_map/all_to_all | solution.py:245
  71.1 0.0 copy-done.1
  71.1 0.0 copy-done.3
  71.1 0.0 copy-done.4
  71.1 1.3 %final.1 = f32[48,96]{1,0:T(8,128)} custom-call(s32[2,64]{1,0:T(2,128)S(1)} %bitcast.11, f32[64]{0:T(128)S(1)} %copy-done.4, f32[8,96]{1,0:T(8,128)S(1)} %reshape.3.vir_ref, f32[48,96]{1,0:T(8,128)S(1)} %bitcast.7, f32[16,48,96]{2,1,0:T(8,128)S(1)} %all-to-all-done.1.ladder_ref, f32[8,48,96]{2,1,0:T(8,128)S(1)} %all-to-all-done.2.hole_ref), custom_call_target="tpu_custom_call" | custom-call | tf_op jit(solution)/shard_map/final/pallas_call | solution.py:247
Async XLA Ops:
  0.0 18.5 %copy-start.2 = (s32[64,2]{0,1:T(2,128)S(1)}, s32[64,2]{0,1:T(2,128)}, u32[]{:S(2)}) copy-start(s32[64,2]{0,1:T(2,128)} %param.9) | copy-start | bytes 1540
  0.0 18.5 %copy-start = (f32[64,64]{1,0:T(8,128)S(1)}, f32[64,64]{1,0:T(8,128)}, u32[]{:S(2)}) copy-start(f32[64,64]{1,0:T(8,128)} %integral_ref.1) | copy-start | bytes 49156
  1.7 16.7 %all-to-all-start = ((f32[8,48,96]{2,1,0:T(8,128)}), f32[8,48,96]{2,1,0:T(8,128)S(1)}, u32[]{:S(2)}, u32[]{:S(2)}) async-start(f32[8,48,96]{2,1,0:T(8,128)} %head.1.after_ref), calls=%async_computation | async-start | bytes 393216 | tf_op jit(solution)/shard_map/all_to_all | solution.py:207
  17.9 38.6 %copy-start.5 = (f32[768]{0:T(1024)S(1)}, f32[768]{0:T(1024)}, u32[]{:S(2)}) copy-start(f32[768]{0:T(1024)} %param.13) | copy-start | bytes 9220
  17.9 53.1 %copy-start.1 = (f32[1,48,96]{2,1,0:T(8,128)S(1)}, f32[1,48,96]{2,1,0:T(8,128)}, u32[]{:S(2)}) copy-start(f32[1,48,96]{2,1,0:T(8,128)} %param.11) | copy-start | bytes 55300
  17.9 53.1 %copy-start.3 = (s32[64,2]{0,1:T(2,128)S(1)}, s32[64,2]{0,1:T(2,128)}, u32[]{:S(2)}) copy-start(s32[64,2]{0,1:T(2,128)} %param.9) | copy-start | bytes 1540
  18.0 53.1 %copy-start.4 = (f32[64]{0:T(128)S(1)}, f32[64]{0:T(128)}, u32[]{:S(2)}) copy-start(f32[64]{0:T(128)} %occ_ref.1) | copy-start | bytes 772
  20.5 25.4 %all-to-all-start.2 = ((f32[8,48,96]{2,1,0:T(8,128)}), f32[8,48,96]{2,1,0:T(8,128)S(1)}, u32[]{:S(2)}, u32[]{:S(2)}) async-start(f32[8,48,96]{2,1,0:T(8,128)} %hole.1.after_ref), calls=%async_computation.2 | async-start | bytes 393216 | tf_op jit(solution)/shard_map/all_to_all | solution.py:246
  45.8 25.2 %all-to-all-start.1 = ((f32[16,48,96]{2,1,0:T(8,128)}), f32[16,48,96]{2,1,0:T(8,128)S(1)}, u32[]{:S(2)}, u32[]{:S(2)}) async-start(f32[16,48,96]{2,1,0:T(8,128)} %ladder.3), calls=%async_computation.1 | async-start | bytes 786432 | tf_op jit(solution)/shard_map/all_to_all | solution.py:245

commit v3 on v2

v3 whole, which is shorter than its diff:
```python
import functools

import jax
import jax.numpy as jnp
from jax import lax
from jax.experimental import pallas as pl
from jax.experimental.pallas import tpu as pltpu
from jax.sharding import PartitionSpec as P

LANES = 128
Y = 8
SIZES = (4, 8, 4)


def split(x):
    high = x.astype(jnp.bfloat16)
    return high, (x - high.astype(jnp.float32)).astype(jnp.bfloat16)


def irrep_of(pair_ref, pair, occ_block):
    return lax.bitwise_xor(
        lax.div(pair_ref[0, pair], occ_block), lax.div(pair_ref[1, pair], occ_block)
    )


def pack(ref, rows):
    height, width = rows.shape
    spare = LANES - width
    ref[:, width:] = jnp.zeros((height - 8, spare), jnp.float32)
    ref[:, :width] = rows[: height - 8]
    for part in range(width // spare):
        ref[part * 8 : part * 8 + 8, width:] = rows[
            height - 8 :, part * spare : (part + 1) * spare
        ]


def unpack(tile, width):
    spare = LANES - width
    last = [tile[part * 8 : part * 8 + 8, width:] for part in range(width // spare)]
    return jnp.concatenate([tile[:, :width], jnp.concatenate(last, axis=1)], axis=0)


def head_kernel(amp_t_ref, mine_ref, window, turned, sem):
    width, rows_all = amp_t_ref.shape
    copies = mine_ref.shape[0]
    rows_dev = mine_ref.shape[1] + 8
    span = window.shape[1]
    first = lax.axis_index("slab") * rows_dev
    base = jnp.minimum(lax.div(first, LANES) * LANES, rows_all - span)
    load = pltpu.make_async_copy(
        amp_t_ref.at[:, pl.ds(pl.multiple_of(base, LANES), span)], window, sem
    )
    load.start()
    load.wait()
    padded = jnp.concatenate(
        [window[...], jnp.zeros((LANES - width, span), jnp.float32)], axis=0
    )
    turned[...] = jnp.transpose(padded)
    rows = turned[pl.ds(pl.multiple_of(first - base, 8), rows_dev), :width]
    for copy in range(copies):
        pack(mine_ref.at[copy], rows)


def ladder_kernel(occ_block, sizes, offset, pair_ref, after_ref, amp_hbm, vec_hbm, *refs):
    base_hbm = refs[0] if offset else None
    out_ref, weight, left_even, left_odd, amp_t, base, vectors, total, sem = refs[-9:]
    _, width, rows_all = vectors.shape
    lefts = (left_even, left_odd)
    starts = [sum(sizes[:c]) for c in range(len(sizes))]
    irrep = irrep_of(pair_ref, lax.axis_index("tile"), occ_block)
    pieces = [(q, 1) for q in range(sizes[0])] + list(zip(starts[1:], sizes[1:]))
    load_amp = pltpu.make_async_copy(amp_hbm, amp_t, sem.at[len(pieces)])
    load_amp.start()
    loads = [
        pltpu.make_async_copy(
            vec_hbm.at[pl.ds(offset + begin, size)], vectors.at[pl.ds(begin, size)], sem.at[index]
        )
        for index, (begin, size) in enumerate(pieces)
    ]
    for load in loads:
        load.start()
    if offset:
        load_base = pltpu.make_async_copy(base_hbm, base, sem.at[len(pieces) + 1])
        load_base.start()
    weight[...] = jnp.zeros_like(weight)
    fill = jnp.zeros((LANES - width, rows_all), jnp.bfloat16)

    def prepare(c, q):
        for half, part in enumerate(split(vectors[starts[c] + q])):
            lefts[c % 2][q, :, half * LANES : (half + 1) * LANES] = jnp.transpose(
                jnp.concatenate([part, fill], axis=0)
            )

    def beside(parts):
        return jnp.concatenate(parts, axis=1)

    def first(c, block):
        size = sizes[c]
        rows = lefts[c % 2][:size, block * width : (block + 1) * width, :]
        both = jnp.dot(
            rows.reshape(size * width, 2 * LANES),
            weight[block],
            preferred_element_type=jnp.float32,
        )
        parts = split(both[:, :LANES] + both[:, LANES:])
        return jnp.concatenate(
            [beside([x[q * width : (q + 1) * width] for q in range(size)]) for x in parts], axis=0
        )

    def second(c, block, middle):
        size = sizes[c]
        begin = pl.multiple_of(lax.bitwise_xor(block, irrep) * width, 16)
        rows = lefts[c % 2][:size, pl.ds(begin, width), :]
        other = jnp.concatenate(
            [
                beside([rows[q, :, h * LANES : (h + 1) * LANES] for q in range(size)])
                for h in range(2)
            ],
            axis=0,
        )
        value = lax.dot_general(
            middle, other, (((1,), (1,)), ((), ())), preferred_element_type=jnp.float32
        )
        total[block] = value if c == 0 else total[block] + value

    load_amp.wait()
    amp = jnp.transpose(amp_t[...])
    for block in range(8):
        high, low = split(amp[block * width : (block + 1) * width, :])
        for row in (0, LANES):
            weight[block, row : row + width, :width] = high
            weight[block, row : row + width, LANES : LANES + width] = low
    for q in range(sizes[0]):
        loads[q].wait()
        prepare(0, q)
    work = [(c, block) for c in range(len(sizes)) for block in range(8)]
    middle = first(*work[0])
    for index, (c, block) in enumerate(work):
        if c + 1 < len(sizes):
            size = sizes[c + 1]
            if block == 0:
                loads[sizes[0] + c].wait()
            for q in range(block * size // 8, (block + 1) * size // 8):
                prepare(c + 1, q)
        following = first(*work[index + 1]) if index + 1 < len(work) else None
        second(c, block, middle)
        middle = following
    if offset:
        load_base.wait()
    half = width // 2
    for block in range(8):
        value = (
            total[block, :width, :width]
            + total[block, :width, width:]
            + total[block, width:, :width]
            + total[block, width:, width:]
        )
        for part in range(2):
            piece = 2 * block + part
            pack(out_ref.at[piece], value[part * half : (part + 1) * half])
            if offset:
                out_ref[piece] = out_ref[piece] + base[piece]


def hole_kernel(occ_block, pair_ref, integral_ref, rows_ref, out_ref):
    me = lax.axis_index("tile")
    my_z, my_y = lax.div(me, Y), lax.rem(me, Y)
    tiles = [rows_ref[y] for y in range(Y)]
    sources = [irrep_of(pair_ref, my_z * Y + y, occ_block) for y in range(Y)]
    for z in range(out_ref.shape[0]):
        target = z * Y + my_y
        irrep = irrep_of(pair_ref, target, occ_block)
        value = None
        for y in range(Y):
            factor = jnp.where(irrep == sources[y], integral_ref[target, my_z * Y + y], 0.0)
            term = factor * tiles[y]
            value = term if value is None else value + term
        out_ref[z] = value


def final_kernel(occ_block, pair_ref, occ_ref, vir_ref, other_ref, ladder_ref, hole_ref, out_ref):
    pair = lax.axis_index("tile")
    slab = lax.axis_index("slab")
    rows, width = out_ref.shape
    irrep = irrep_of(pair_ref, pair, occ_block)
    block = lax.div(slab, 2)
    moved = ladder_ref[0]
    for piece in range(1, ladder_ref.shape[0]):
        moved = moved + ladder_ref[piece]
    for piece in range(hole_ref.shape[0]):
        moved = moved + hole_ref[piece]
    residual = other_ref[...] + unpack(moved, width)
    pair_energy = occ_ref[pair_ref[0, pair]] + occ_ref[pair_ref[1, pair]]
    column = vir_ref[pl.ds(lax.bitwise_xor(block, irrep), 1), :]
    own = vir_ref[pl.ds(block, 1), :]
    lane = lax.broadcasted_iota(jnp.int32, (rows, width), 1)
    row = lax.broadcasted_iota(jnp.int32, (rows, width), 0) + lax.rem(slab, 2) * rows
    row_energy = jnp.sum(jnp.where(lane == row, own, 0.0), axis=1, keepdims=True)
    out_ref[...] = residual / (pair_energy - row_energy - column)


def local(amplitudes, cholesky, pair_occ, hole_integrals, other_terms, occ_energy, vir_energy):
    _, rows_all, width = amplitudes.shape
    vectors = cholesky.shape[0]
    slabs = lax.axis_size("slab")
    tiles = lax.axis_size("tile")
    rows_dev = rows_all // slabs
    depth = tiles // Y
    packed = (rows_dev - 8, LANES)
    occ_block = occ_energy.shape[0] // 8
    vmem = pl.BlockSpec(memory_space=pltpu.VMEM)
    smem = pl.BlockSpec(memory_space=pltpu.SMEM)
    groups_y = [[z * Y + y for y in range(Y)] for z in range(depth)]
    groups_z = [[z * Y + y for z in range(depth)] for y in range(Y)]

    hbm = pl.BlockSpec(memory_space=pltpu.MemorySpace.HBM)
    small = pltpu.CompilerParams(vmem_limit_bytes=6 << 20)
    pairs = jnp.transpose(pair_occ)
    amp_t = jnp.transpose(amplitudes[0])
    vectors_t = jnp.transpose(cholesky, (0, 2, 1))

    mine = pl.pallas_call(
        head_kernel,
        out_shape=jax.ShapeDtypeStruct((Y,) + packed, jnp.float32),
        in_specs=[hbm],
        out_specs=vmem,
        scratch_shapes=[
            pltpu.VMEM((width, 2 * LANES), jnp.float32),
            pltpu.VMEM((2 * LANES, LANES), jnp.float32),
            pltpu.SemaphoreType.DMA,
        ],
        compiler_params=pltpu.CompilerParams(vmem_limit_bytes=60 << 20),
        name="head",
    )(amp_t)
    gathered = lax.all_to_all(mine, "tile", 0, 0, axis_index_groups=groups_y, tiled=True)

    sizes = SIZES
    share = vectors // 2

    def ladder_part(offset, after, *base):
        flops = 2 * share * 8 * width * (2 * LANES) * (2 * LANES) * 2
        return pl.pallas_call(
            functools.partial(ladder_kernel, occ_block, sizes, offset),
            out_shape=jax.ShapeDtypeStruct((slabs,) + packed, jnp.float32),
            in_specs=[smem, hbm, hbm, hbm] + [hbm] * len(base),
            out_specs=vmem,
            scratch_shapes=[
                pltpu.VMEM((8, 2 * LANES, 2 * LANES), jnp.bfloat16),
                pltpu.VMEM((max(sizes[::2]), rows_all, 2 * LANES), jnp.bfloat16),
                pltpu.VMEM((max(sizes[1::2]), rows_all, 2 * LANES), jnp.bfloat16),
                pltpu.VMEM((width, rows_all), jnp.float32),
                pltpu.VMEM((slabs,) + packed, jnp.float32),
                pltpu.VMEM((share, width, rows_all), jnp.float32),
                pltpu.VMEM((8, 2 * width, 2 * width), jnp.float32),
                pltpu.SemaphoreType.DMA((sizes[0] + len(sizes) + 1,)),
            ],
            compiler_params=pltpu.CompilerParams(vmem_limit_bytes=58 << 20),
            cost_estimate=pl.CostEstimate(
                flops=flops, bytes_accessed=share * rows_all * width * 4, transcendentals=0
            ),
            name="ladder",
        )(pairs, after, amp_t, vectors_t, *base)

    ladder = ladder_part(0, mine)
    gathered, ladder = lax.optimization_barrier((gathered, ladder))
    partial = pl.pallas_call(
        functools.partial(hole_kernel, occ_block),
        out_shape=jax.ShapeDtypeStruct((depth,) + packed, jnp.float32),
        in_specs=[smem, smem, vmem],
        out_specs=vmem,
        compiler_params=small,
        name="hole",
    )(pairs, hole_integrals, gathered)
    ladder = ladder_part(share, partial, ladder)
    vir = vir_energy.reshape(8, width)
    ladder, vir = lax.optimization_barrier((ladder, vir))
    pieces = lax.all_to_all(ladder, "slab", 0, 0, tiled=True)
    hole = lax.all_to_all(partial, "tile", 0, 0, axis_index_groups=groups_z, tiled=True)
    out = pl.pallas_call(
        functools.partial(final_kernel, occ_block),
        out_shape=jax.ShapeDtypeStruct((rows_dev, width), jnp.float32),
        in_specs=[smem, smem, vmem, vmem, vmem, vmem],
        out_specs=vmem,
        compiler_params=small,
        name="final",
    )(pairs, occ_energy, vir, other_terms[0], pieces, hole)
    return out[None]


def solution(mesh):
    placed = (
        P("tile", None, None),
        P("slab", None, None),
        P(),
        P(),
        P("tile", "slab", None),
        P(),
        P(),
    )
    return jax.shard_map(
        local, mesh=mesh, in_specs=placed, out_specs=P("tile", "slab", None), check_vma=False
    )
```

time: 72.8 us -> 70.3 us (0.966)
  blocking collectives: 0 us -> 23 us
  waiting for transfers between devices: 15.5 us -> 0.01 us
  starting transfers between devices: 35.4 us -> 24.5 us
    all_to_all x0 -> x1, blocking collectives: none -> 23 us  [local(): pieces = lax.all_to_all(ladder, 'slab', 0, 0, tiled=True)]
    all_to_all x1 -> x0, waiting for transfers between devices: 14.5 us -> none  [local(): pieces = lax.all_to_all(ladder, 'slab', 0, 0, tiled=True)]
    all_to_all x1 -> x0, starting transfers between devices: 10.7 us -> none  [local(): pieces = lax.all_to_all(ladder, 'slab', 0, 0, tiled=True)]
  transfers between devices with their start and end apart: 3 -> 2, of which waited for: 3 -> 0; matrix products, arithmetic and copies ran while one was open for 0% -> 1% of each run, Pallas kernels for 23% -> 23%
where the time goes in v3:
time: 70.3 us; the launch traced here: 69.8 us
  starting transfers between devices  24.5 us (35%)
  blocking collectives  23 us (33%)
  Pallas kernels  21.4 us (30%)
  local copies, waits for them, and re-layouts  0.78 us (1%)
    all_to_all x1, blocking collectives, local(): pieces = lax.all_to_all(ladder, 'slab', 0, 0, tiled=True)  23 us
    all_to_all x1, starting transfers between devices, local(): lax.all_to_all(partial, 'tile', 0, 0, axis_index_groups=groups_z, tiled=T...  16.4 us
    pallas_call x2, Pallas kernels, ladder_part(): pl.pallas_call(functools.partial(ladder_kernel, occ_block, sizes, offset)...  16.4 us
    all_to_all x1, starting transfers between devices, local(): lax.all_to_all(mine, 'tile', 0, 0, axis_index_groups=groups_y, tiled=True)  8.12 us
    pallas_call x1, Pallas kernels, local(): pl.pallas_call(functools.partial(hole_kernel, occ_block), out_shape=jax.S...  1.99 us
    pallas_call x1, Pallas kernels, local(): pl.pallas_call(head_kernel, out_shape=jax.ShapeDtypeStruct((Y,) + packed,...  1.76 us
  transfers between devices with their start and end apart: 2, of which 0 were waited for; matrix products, arithmetic and copies ran while one was open for 1% of the time, Pallas kernels for 23%

profile of v3, /device:TPU:1, one launch (start us, length us, event | category | flops | bytes accessed | tf_op | source)
XLA Modules:
  0.0 69.8 jit_solution(16738009611663147044)
XLA Ops:
  0.0 0.0 copy-start.2
  0.0 0.0 copy-start
  0.0 1.8 %head.1.after_ref = f32[8,40,128]{2,1,0:T(8,128)} custom-call(f32[96,768]{1,0:T(8,128)} %bitcast.12), custom_call_target="tpu_custom_call" | custom-call | tf_op jit(solution)/shard_map/head/pallas_call | solution.py:222
  1.8 8.1 %all-to-all-start = ((f32[8,40,128]{2,1,0:T(8,128)}), f32[8,40,128]{2,1,0:T(8,128)S(1)}, u32[]{:S(2)}, u32[]{:S(2)}) async-start(f32[8,40,128]{2,1,0:T(8,128)} %head.1.after_ref), calls=%async_computation | async-start | bytes 327680 | tf_op jit(solution)/shard_map/all_to_all | solution.py:235
  9.9 0.8 %reshape.3.vir_ref = f32[8,96]{1,0:T(8,128)S(1)} reshape(f32[768]{0:T(1024)} %param.13) | data formatting | bytes 6144 | tf_op jit(solution)/shard_map/reshape | solution.py:275
  10.6 7.8 %ladder.2.refs_0_ = f32[16,40,128]{2,1,0:T(8,128)} custom-call(s32[2,64]{1,0:T(2,128)} %bitcast.8, f32[8,40,128]{2,1,0:T(8,128)} %head.1.after_ref, f32[96,768]{1,0:T(8,128)} %bitcast.13, f32[32,96,768]{2,1,0:T(8,128)} %bitcast.15), custom_call_target="tpu_custom_call" | custom-call | flops 3221225472 | bytes 4718592 | tf_op jit(solution)/shard_map/ladder/pallas_call | solution.py:242
  18.5 0.0 copy-start.1
  18.5 0.0 copy-start.3
  18.5 0.0 copy-start.4
  18.5 0.0 all-to-all-done.rows_ref
  18.5 0.0 copy-done.2
  18.5 0.0 copy-done
  18.5 2.0 %hole.1.after_ref = f32[8,40,128]{2,1,0:T(8,128)} custom-call(s32[2,64]{1,0:T(2,128)S(1)} %bitcast.10, f32[64,64]{1,0:T(8,128)S(1)} %copy-done, f32[8,40,128]{2,1,0:T(8,128)S(1)} %all-to-all-done.rows_ref), custom_call_target="tpu_custom_call" | custom-call | tf_op jit(solution)/shard_map/hole/pallas_call | solution.py:266
  20.5 16.4 %all-to-all-start.2 = ((f32[8,40,128]{2,1,0:T(8,128)}), f32[8,40,128]{2,1,0:T(8,128)S(1)}, u32[]{:S(2)}, u32[]{:S(2)}) async-start(f32[8,40,128]{2,1,0:T(8,128)} %hole.1.after_ref), calls=%async_computation.2 | async-start | bytes 327680 | tf_op jit(solution)/shard_map/all_to_all | solution.py:278
  36.9 8.6 %ladder.3 = f32[16,40,128]{2,1,0:T(8,128)} custom-call(s32[2,64]{1,0:T(2,128)} %bitcast.9, f32[8,40,128]{2,1,0:T(8,128)} %hole.1.after_ref, f32[96,768]{1,0:T(8,128)} %bitcast.14, f32[32,96,768]{2,1,0:T(8,128)} %bitcast.16, f32[16,40,128]{2,1,0:T(8,128)} %ladder.2.refs_0_), custom_call_target="tpu_custom_call" | custom-call | flops 3221225472 | bytes 4718592 | tf_op jit(solution)/shard_map/ladder/pallas_call | solution.py:242
  45.5 0.0 all-to-all-done.2.hole_ref
  45.5 23.0 %all_to_all.15.ladder_ref = f32[16,40,128]{2,1,0:T(8,128)S(1)} all-to-all(f32[16,40,128]{2,1,0:T(8,128)} %ladder.3), channel_id=1, replica_groups=mesh['tile'=64,'slab'=16] {'slab'}, dimensions={0} | all-to-all | bytes 655360 | tf_op jit(solution)/shard_map/all_to_all | solution.py:277
  68.6 0.0 copy-done.1
  68.6 0.0 copy-done.3
  68.6 0.0 copy-done.4
  68.6 1.3 %final.1 = f32[48,96]{1,0:T(8,128)} custom-call(s32[2,64]{1,0:T(2,128)S(1)} %bitcast.11, f32[64]{0:T(128)S(1)} %copy-done.4, f32[8,96]{1,0:T(8,128)S(1)} %reshape.3.vir_ref, f32[48,96]{1,0:T(8,128)S(1)} %bitcast.7, f32[16,40,128]{2,1,0:T(8,128)S(1)} %all_to_all.15.ladder_ref, f32[8,40,128]{2,1,0:T(8,128)S(1)} %all-to-all-done.2.hole_ref), custom_call_target="tpu_custom_call" | custom-call | tf_op jit(solution)/shard_map/final/pallas_call | solution.py:279
Async XLA Ops:
  0.0 18.5 %copy-start.2 = (s32[64,2]{0,1:T(2,128)S(1)}, s32[64,2]{0,1:T(2,128)}, u32[]{:S(2)}) copy-start(s32[64,2]{0,1:T(2,128)} %param.9) | copy-start | bytes 1540
  0.0 18.5 %copy-start = (f32[64,64]{1,0:T(8,128)S(1)}, f32[64,64]{1,0:T(8,128)}, u32[]{:S(2)}) copy-start(f32[64,64]{1,0:T(8,128)} %integral_ref.1) | copy-start | bytes 49156
  1.8 16.7 %all-to-all-start = ((f32[8,40,128]{2,1,0:T(8,128)}), f32[8,40,128]{2,1,0:T(8,128)S(1)}, u32[]{:S(2)}, u32[]{:S(2)}) async-start(f32[8,40,128]{2,1,0:T(8,128)} %head.1.after_ref), calls=%async_computation | async-start | bytes 327680 | tf_op jit(solution)/shard_map/all_to_all | solution.py:235
  18.5 50.1 %copy-start.1 = (f32[1,48,96]{2,1,0:T(8,128)S(1)}, f32[1,48,96]{2,1,0:T(8,128)}, u32[]{:S(2)}) copy-start(f32[1,48,96]{2,1,0:T(8,128)} %param.11) | copy-start | bytes 55300
  18.5 50.1 %copy-start.3 = (s32[64,2]{0,1:T(2,128)S(1)}, s32[64,2]{0,1:T(2,128)}, u32[]{:S(2)}) copy-start(s32[64,2]{0,1:T(2,128)} %param.9) | copy-start | bytes 1540
  18.5 50.1 %copy-start.4 = (f32[64]{0:T(128)S(1)}, f32[64]{0:T(128)}, u32[]{:S(2)}) copy-start(f32[64]{0:T(128)} %occ_ref.1) | copy-start | bytes 772
  20.5 25.0 %all-to-all-start.2 = ((f32[8,40,128]{2,1,0:T(8,128)}), f32[8,40,128]{2,1,0:T(8,128)S(1)}, u32[]{:S(2)}, u32[]{:S(2)}) async-start(f32[8,40,128]{2,1,0:T(8,128)} %hole.1.after_ref), calls=%async_computation.2 | async-start | bytes 327680 | tf_op jit(solution)/shard_map/all_to_all | solution.py:278

commit v4 on v3

--- a/solution.py
+++ b/solution.py
@@ -9,7 +9,8 @@
 
 LANES = 128
 Y = 8
-SIZES = (4, 8, 4)
+SIZES = (2, 6, 8, 8, 8)
+CLASSES = 4
 
 
 def split(x):
@@ -61,9 +62,10 @@
         pack(mine_ref.at[copy], rows)
 
 
-def ladder_kernel(occ_block, sizes, offset, pair_ref, after_ref, amp_hbm, vec_hbm, *refs):
-    base_hbm = refs[0] if offset else None
-    out_ref, weight, left_even, left_odd, amp_t, base, vectors, total, sem = refs[-9:]
+def ladder_kernel(
+    occ_block, sizes, pair_ref, after_ref, amp_hbm, vec_hbm, out_ref,
+    weight, left_even, left_odd, amp_t, vectors, total, sem,
+):
     _, width, rows_all = vectors.shape
     lefts = (left_even, left_odd)
     starts = [sum(sizes[:c]) for c in range(len(sizes))]
@@ -73,15 +75,12 @@
     load_amp.start()
     loads = [
         pltpu.make_async_copy(
-            vec_hbm.at[pl.ds(offset + begin, size)], vectors.at[pl.ds(begin, size)], sem.at[index]
+            vec_hbm.at[pl.ds(begin, size)], vectors.at[pl.ds(begin, size)], sem.at[index]
         )
         for index, (begin, size) in enumerate(pieces)
     ]
     for load in loads:
         load.start()
-    if offset:
-        load_base = pltpu.make_async_copy(base_hbm, base, sem.at[len(pieces) + 1])
-        load_base.start()
     weight[...] = jnp.zeros_like(weight)
     fill = jnp.zeros((LANES - width, rows_all), jnp.bfloat16)
 
@@ -145,8 +144,6 @@
         following = first(*work[index + 1]) if index + 1 < len(work) else None
         second(c, block, middle)
         middle = following
-    if offset:
-        load_base.wait()
     half = width // 2
     for block in range(8):
         value = (
@@ -158,27 +155,28 @@
         for part in range(2):
             piece = 2 * block + part
             pack(out_ref.at[piece], value[part * half : (part + 1) * half])
-            if offset:
-                out_ref[piece] = out_ref[piece] + base[piece]
-
-
-def hole_kernel(occ_block, pair_ref, integral_ref, rows_ref, out_ref):
+
+
+def hole_kernel(occ_block, pair_ref, integral_ref, rows_ref, *out_refs):
     me = lax.axis_index("tile")
     my_z, my_y = lax.div(me, Y), lax.rem(me, Y)
-    tiles = [rows_ref[y] for y in range(Y)]
-    sources = [irrep_of(pair_ref, my_z * Y + y, occ_block) for y in range(Y)]
-    for z in range(out_ref.shape[0]):
-        target = z * Y + my_y
+    low = lax.rem(my_z, CLASSES)
+    count = rows_ref.shape[0]
+    sources = [(low + CLASSES * (i // Y)) * Y + i % Y for i in range(count)]
+    irreps = [irrep_of(pair_ref, source, occ_block) for source in sources]
+    for step, out_ref in enumerate(out_refs):
+        target = lax.bitwise_xor(my_z, step) * Y + my_y
         irrep = irrep_of(pair_ref, target, occ_block)
         value = None
-        for y in range(Y):
-            factor = jnp.where(irrep == sources[y], integral_ref[target, my_z * Y + y], 0.0)
-            term = factor * tiles[y]
+        for i in range(count):
+            factor = jnp.where(irrep == irreps[i], integral_ref[target, sources[i]], 0.0)
+            term = factor * rows_ref[i]
             value = term if value is None else value + term
-        out_ref[z] = value
-
-
-def final_kernel(occ_block, pair_ref, occ_ref, vir_ref, other_ref, ladder_ref, hole_ref, out_ref):
+        out_ref[...] = value
+
+
+def final_kernel(occ_block, pair_ref, occ_ref, vir_ref, other_ref, ladder_ref, *refs):
+    out_ref = refs[-1]
     pair = lax.axis_index("tile")
     slab = lax.axis_index("slab")
     rows, width = out_ref.shape
@@ -187,8 +185,8 @@
     moved = ladder_ref[0]
     for piece in range(1, ladder_ref.shape[0]):
         moved = moved + ladder_ref[piece]
-    for piece in range(hole_ref.shape[0]):
-        moved = moved + hole_ref[piece]
+    for hole_ref in refs[:-1]:
+        moved = moved + hole_ref[...]
     residual = other_ref[...] + unpack(moved, width)
     pair_energy = occ_ref[pair_ref[0, pair]] + occ_ref[pair_ref[1, pair]]
     column = vir_ref[pl.ds(lax.bitwise_xor(block, irrep), 1), :]
@@ -210,8 +208,11 @@
     occ_block = occ_energy.shape[0] // 8
     vmem = pl.BlockSpec(memory_space=pltpu.VMEM)
     smem = pl.BlockSpec(memory_space=pltpu.SMEM)
-    groups_y = [[z * Y + y for y in range(Y)] for z in range(depth)]
-    groups_z = [[z * Y + y for z in range(depth)] for y in range(Y)]
+    spread = depth // CLASSES
+    groups = [
+        [(low + CLASSES * far) * Y + y for far in range(spread) for y in range(Y)]
+        for low in range(CLASSES)
+    ]
 
     hbm = pl.BlockSpec(memory_space=pltpu.MemorySpace.HBM)
     small = pltpu.CompilerParams(vmem_limit_bytes=6 << 20)
@@ -221,7 +222,7 @@
 
     mine = pl.pallas_call(
         head_kernel,
-        out_shape=jax.ShapeDtypeStruct((Y,) + packed, jnp.float32),
+        out_shape=jax.ShapeDtypeStruct((spread * Y,) + packed, jnp.float32),
         in_specs=[hbm],
         out_specs=vmem,
         scratch_shapes=[
@@ -232,58 +233,52 @@
         compiler_params=pltpu.CompilerParams(vmem_limit_bytes=60 << 20),
         name="head",
     )(amp_t)
-    gathered = lax.all_to_all(mine, "tile", 0, 0, axis_index_groups=groups_y, tiled=True)
+    gathered = lax.all_to_all(mine, "tile", 0, 0, axis_index_groups=groups, tiled=True)
 
     sizes = SIZES
-    share = vectors // 2
-
-    def ladder_part(offset, after, *base):
-        flops = 2 * share * 8 * width * (2 * LANES) * (2 * LANES) * 2
-        return pl.pallas_call(
-            functools.partial(ladder_kernel, occ_block, sizes, offset),
-            out_shape=jax.ShapeDtypeStruct((slabs,) + packed, jnp.float32),
-            in_specs=[smem, hbm, hbm, hbm] + [hbm] * len(base),
-            out_specs=vmem,
-            scratch_shapes=[
-                pltpu.VMEM((8, 2 * LANES, 2 * LANES), jnp.bfloat16),
-                pltpu.VMEM((max(sizes[::2]), rows_all, 2 * LANES), jnp.bfloat16),
-                pltpu.VMEM((max(sizes[1::2]), rows_all, 2 * LANES), jnp.bfloat16),
-                pltpu.VMEM((width, rows_all), jnp.float32),
-                pltpu.VMEM((slabs,) + packed, jnp.float32),
-                pltpu.VMEM((share, width, rows_all), jnp.float32),
-                pltpu.VMEM((8, 2 * width, 2 * width), jnp.float32),
-                pltpu.SemaphoreType.DMA((sizes[0] + len(sizes) + 1,)),
-            ],
-            compiler_params=pltpu.CompilerParams(vmem_limit_bytes=58 << 20),
-            cost_estimate=pl.CostEstimate(
-                flops=flops, bytes_accessed=share * rows_all * width * 4, transcendentals=0
-            ),
-            name="ladder",
-        )(pairs, after, amp_t, vectors_t, *base)
-
-    ladder = ladder_part(0, mine)
-    gathered, ladder = lax.optimization_barrier((gathered, ladder))
+    flops = 2 * vectors * 8 * width * (2 * LANES) * (2 * LANES) * 2
+    ladder = pl.pallas_call(
+        functools.partial(ladder_kernel, occ_block, sizes),
+        out_shape=jax.ShapeDtypeStruct((slabs,) + packed, jnp.float32),
+        in_specs=[smem, hbm, hbm, hbm],
+        out_specs=vmem,
+        scratch_shapes=[
+            pltpu.VMEM((8, 2 * LANES, 2 * LANES), jnp.bfloat16),
+            pltpu.VMEM((max(sizes[::2]), rows_all, 2 * LANES), jnp.bfloat16),
+            pltpu.VMEM((max(sizes[1::2]), rows_all, 2 * LANES), jnp.bfloat16),
+            pltpu.VMEM((width, rows_all), jnp.float32),
+            pltpu.VMEM((vectors, width, rows_all), jnp.float32),
+            pltpu.VMEM((8, 2 * width, 2 * width), jnp.float32),
+            pltpu.SemaphoreType.DMA((sizes[0] + len(sizes),)),
+        ],
+        compiler_params=pltpu.CompilerParams(vmem_limit_bytes=58 << 20),
+        cost_estimate=pl.CostEstimate(
+            flops=flops, bytes_accessed=cholesky.size * 4, transcendentals=0
+        ),
+        name="ladder",
+    )(pairs, mine, amp_t, vectors_t)
+    pieces = lax.all_to_all(ladder, "slab", 0, 0, tiled=True)
+    gathered, _ = lax.optimization_barrier((gathered, ladder))
     partial = pl.pallas_call(
         functools.partial(hole_kernel, occ_block),
-        out_shape=jax.ShapeDtypeStruct((depth,) + packed, jnp.float32),
+        out_shape=[jax.ShapeDtypeStruct(packed, jnp.float32)] * CLASSES,
         in_specs=[smem, smem, vmem],
-        out_specs=vmem,
+        out_specs=[vmem] * CLASSES,
         compiler_params=small,
         name="hole",
     )(pairs, hole_integrals, gathered)
-    ladder = ladder_part(share, partial, ladder)
-    vir = vir_energy.reshape(8, width)
-    ladder, vir = lax.optimization_barrier((ladder, vir))
-    pieces = lax.all_to_all(ladder, "slab", 0, 0, tiled=True)
-    hole = lax.all_to_all(partial, "tile", 0, 0, axis_index_groups=groups_z, tiled=True)
+    hole = [partial[0]]
+    for step in range(1, CLASSES):
+        route = [(z * Y + y, (z ^ step) * Y + y) for z in range(depth) for y in range(Y)]
+        hole.append(lax.ppermute(partial[step], "tile", route))
     out = pl.pallas_call(
         functools.partial(final_kernel, occ_block),
         out_shape=jax.ShapeDtypeStruct((rows_dev, width), jnp.float32),
-        in_specs=[smem, smem, vmem, vmem, vmem, vmem],
+        in_specs=[smem, smem] + [vmem] * (3 + CLASSES),
         out_specs=vmem,
         compiler_params=small,
         name="final",
-    )(pairs, occ_energy, vir, other_terms[0], pieces, hole)
+    )(pairs, occ_energy, vir_energy.reshape(8, width), other_terms[0], pieces, *hole)
     return out[None]
 
 

time: 70.3 us -> 65.2 us (0.927)
  blocking collectives: 23 us -> 0 us
  starting transfers between devices: 24.5 us -> 41.2 us
  waiting for transfers between devices: 0.01 us -> 6.72 us
  Pallas kernels: 21.4 us -> 15.9 us
    all_to_all x1 -> x0, blocking collectives: 23 us -> none  [local(): pieces = lax.all_to_all(ladder, 'slab', 0, 0, tiled=True)]
    ppermute x0 -> x3, starting transfers between devices: none -> 11.6 us  [local(): hole.append(lax.ppermute(partial[step], 'tile', route))]
    pallas_call x4 -> x3, Pallas kernels: 20.1 us -> 14.6 us  [the longest x1 11.4 us: local(): pl.pallas_call(functools.partial(ladder_kernel, occ_block, sizes), out_sh...]
    all_to_all x2, starting transfers between devices: 24.5 us -> 29.7 us  [the longest x1 20.3 us: local(): lax.all_to_all(mine, 'tile', 0, 0, axis_index_groups=groups, tiled=True)]
    ppermute x0 -> x3, waiting for transfers between devices: none -> 4.3 us  [local(): hole.append(lax.ppermute(partial[step], 'tile', route))]
    all_to_all x2, waiting for transfers between devices: 0.01 us -> 2.42 us  [the longest x1 2.42 us: local(): lax.all_to_all(mine, 'tile', 0, 0, axis_index_groups=groups, tiled=True)]
  transfers between devices with their start and end apart: 2 -> 5, of which waited for: 0 -> 2; matrix products, arithmetic and copies ran while one was open for 1% -> 0% of each run, Pallas kernels for 23% -> 20%
where the time goes in v4:
time: 65.2 us; the launch traced here: 64 us
  starting transfers between devices  41.2 us (63%)
  Pallas kernels  15.9 us (24%)
  waiting for transfers between devices  6.72 us (10%)
    all_to_all x1, starting transfers between devices, local(): lax.all_to_all(mine, 'tile', 0, 0, axis_index_groups=groups, tiled=True)  20.3 us
    ppermute x3, starting transfers between devices, local(): hole.append(lax.ppermute(partial[step], 'tile', route))  11.6 us
    pallas_call x1, Pallas kernels, local(): pl.pallas_call(functools.partial(ladder_kernel, occ_block, sizes), out_sh...  11.4 us
    all_to_all x1, starting transfers between devices, local(): pieces = lax.all_to_all(ladder, 'slab', 0, 0, tiled=True)  9.36 us
    ppermute x3, waiting for transfers between devices, local(): hole.append(lax.ppermute(partial[step], 'tile', route))  4.3 us
    all_to_all x1, waiting for transfers between devices, local(): lax.all_to_all(mine, 'tile', 0, 0, axis_index_groups=groups, tiled=True)  2.42 us
    pallas_call x1, Pallas kernels, local(): pl.pallas_call(head_kernel, out_shape=jax.ShapeDtypeStruct((spread * Y,)...  1.8 us
    pallas_call x1, Pallas kernels, local(): pl.pallas_call(functools.partial(hole_kernel, occ_block), out_shape=[jax....  1.38 us
  transfers between devices with their start and end apart: 5, of which 2 were waited for; matrix products, arithmetic and copies ran while one was open for 0% of the time, Pallas kernels for 20%

profile of v4, /device:TPU:1, one launch (start us, length us, event | category | flops | bytes accessed | tf_op | source)
XLA Modules:
  0.0 64.0 jit_solution(16455372729936697982)
XLA Ops:
  0.0 1.8 %head.1.after_ref = f32[16,40,128]{2,1,0:T(8,128)} custom-call(f32[96,768]{1,0:T(8,128)} %bitcast.11), custom_call_target="tpu_custom_call" | custom-call | tf_op jit(solution)/shard_map/head/pallas_call | solution.py:223
  1.8 20.3 %all-to-all-start.1 = ((f32[16,40,128]{2,1,0:T(8,128)}), f32[16,40,128]{2,1,0:T(8,128)S(1)}, u32[]{:S(2)}, u32[]{:S(2)}) async-start(f32[16,40,128]{2,1,0:T(8,128)} %head.1.after_ref), calls=%async_computation.1 | async-start | bytes 655360 | tf_op jit(solution)/shard_map/all_to_all | solution.py:236
  22.1 0.0 copy-start
  22.1 0.0 copy-start.2
  22.1 0.0 copy-start.4
  22.2 0.0 copy-start.1
  22.2 0.0 copy-start.3
  22.2 11.4 %ladder.1 = f32[16,40,128]{2,1,0:T(8,128)} custom-call(s32[2,64]{1,0:T(2,128)} %bitcast.8, f32[16,40,128]{2,1,0:T(8,128)} %head.1.after_ref, f32[96,768]{1,0:T(8,128)} %bitcast.12, f32[32,96,768]{2,1,0:T(8,128)} %bitcast.13), custom_call_target="tpu_custom_call" | custom-call | flops 6442450944 | bytes 9437184 | tf_op jit(solution)/shard_map/ladder/pallas_call | solution.py:240
  33.6 2.4 %all-to-all-done.1.rows_ref = f32[16,40,128]{2,1,0:T(8,128)S(1)} async-done(((f32[16,40,128]{2,1,0:T(8,128)}), f32[16,40,128]{2,1,0:T(8,128)S(1)}, u32[]{:S(2)}, u32[]{:S(2)}) %all-to-all-start.1) | async-done | bytes 327712 | tf_op jit(solution)/shard_map/all_to_all | solution.py:236
  36.0 9.4 %all-to-all-start = ((f32[16,40,128]{2,1,0:T(8,128)}), f32[16,40,128]{2,1,0:T(8,128)S(1)}, u32[]{:S(2)}, u32[]{:S(2)}) async-start(f32[16,40,128]{2,1,0:T(8,128)} %ladder.1), calls=%async_computation | async-start | bytes 655360 | tf_op jit(solution)/shard_map/all_to_all | solution.py:260
  45.4 0.0 copy-done
  45.4 0.0 copy-done.2
  45.4 1.4 %hole.1 = (f32[40,128]{1,0:T(8,128)S(1)}, f32[40,128]{1,0:T(8,128)S(1)}, f32[40,128]{1,0:T(8,128)S(1)}, f32[40,128]{1,0:T(8,128)S(1)}) custom-call(s32[2,64]{1,0:T(2,128)S(1)} %bitcast.9, f32[64,64]{1,0:T(8,128)S(1)} %copy-done, f32[16,40,128]{2,1,0:T(8,128)S(1)} %all-to-all-done.1.rows_ref), custom_call_target="tpu_custom_call" | custom-call | tf_op jit(solution)/shard_map/hole/pallas_call | solution.py:262
  46.8 3.8 %collective-permute-start = (f32[40,128]{1,0:T(8,128)S(1)}, f32[40,128]{1,0:T(8,128)S(1)}, u32[]{:S(2)}, u32[]{:S(2)}) collective-permute-start(f32[40,128]{1,0:T(8,128)S(1)} %get-tuple-element.12), channel_id=1, source_target_pairs={{0,128},{16,144},{32,160},{48,176},{64,192},{80,208},{96,224},{112... | collective-permute-start | bytes 61448 | tf_op jit(solution)/shard_map/ppermute | solution.py:273
  50.6 5.8 %collective-permute-start.1 = (f32[40,128]{1,0:T(8,128)S(1)}, f32[40,128]{1,0:T(8,128)S(1)}, u32[]{:S(2)}, u32[]{:S(2)}) collective-permute-start(f32[40,128]{1,0:T(8,128)S(1)} %get-tuple-element.13), channel_id=1, source_target_pairs={{0,256},{16,272},{32,288},{48,304},{64,320},{80,336},{96,352},{112... | collective-permute-start | bytes 61448 | tf_op jit(solution)/shard_map/ppermute | solution.py:273
  56.4 1.9 %collective-permute-start.2 = (f32[40,128]{1,0:T(8,128)S(1)}, f32[40,128]{1,0:T(8,128)S(1)}, u32[]{:S(2)}, u32[]{:S(2)}) collective-permute-start(f32[40,128]{1,0:T(8,128)S(1)} %get-tuple-element.14), channel_id=1, source_target_pairs={{0,384},{16,400},{32,416},{48,432},{64,448},{80,464},{96,480},{112... | collective-permute-start | bytes 61448 | tf_op jit(solution)/shard_map/ppermute | solution.py:273
  58.4 0.0 copy-done.4
  58.4 0.1 reshape.3.vir_ref
  58.5 0.0 all-to-all-done.ladder_ref
  58.5 0.0 collective-permute-done.refs_1_
  58.5 0.0 collective-permute-done.1.refs_2_
  58.5 4.3 %collective-permute-done.2.refs_3_ = f32[40,128]{1,0:T(8,128)S(1)} collective-permute-done((f32[40,128]{1,0:T(8,128)S(1)}, f32[40,128]{1,0:T(8,128)S(1)}, u32[]{:S(2)}, u32[]{:S(2)}) %collective-permute-start.2) | collective-permute-done | bytes 20512 | tf_op jit(solution)/shard_map/ppermute | solution.py:273
  62.8 0.0 copy-done.1
  62.8 0.0 copy-done.3
  62.8 1.3 %final.1 = f32[48,96]{1,0:T(8,128)} custom-call(s32[2,64]{1,0:T(2,128)S(1)} %bitcast.10, f32[64]{0:T(128)S(1)} %copy-done.3, f32[8,96]{1,0:T(8,128)S(1)} %reshape.3.vir_ref, f32[48,96]{1,0:T(8,128)S(1)} %bitcast.7, f32[16,40,128]{2,1,0:T(8,128)S(1)} %all-to-all-done.ladder_ref, f32[40,128]{1,0:T(8,128)S(1)} %get-tuple-element.11.refs_0_, ...), custom_call_target="tpu_custom_call" | custom-call | tf_op jit(solution)/shard_map/final/pallas_call | solution.py:274
Async XLA Ops:
  1.8 34.2 %all-to-all-start.1 = ((f32[16,40,128]{2,1,0:T(8,128)}), f32[16,40,128]{2,1,0:T(8,128)S(1)}, u32[]{:S(2)}, u32[]{:S(2)}) async-start(f32[16,40,128]{2,1,0:T(8,128)} %head.1.after_ref), calls=%async_computation.1 | async-start | bytes 655360 | tf_op jit(solution)/shard_map/all_to_all | solution.py:236
  22.1 23.3 %copy-start = (f32[64,64]{1,0:T(8,128)S(1)}, f32[64,64]{1,0:T(8,128)}, u32[]{:S(2)}) copy-start(f32[64,64]{1,0:T(8,128)} %integral_ref.1) | copy-start | bytes 49156
  22.1 23.3 %copy-start.2 = (s32[64,2]{0,1:T(2,128)S(1)}, s32[64,2]{0,1:T(2,128)}, u32[]{:S(2)}) copy-start(s32[64,2]{0,1:T(2,128)} %param.9) | copy-start | bytes 1540
  22.1 36.2 %copy-start.4 = (f32[768]{0:T(1024)S(1)}, f32[768]{0:T(1024)}, u32[]{:S(2)}) copy-start(f32[768]{0:T(1024)} %param.13) | copy-start | bytes 9220
  22.2 40.6 %copy-start.1 = (f32[1,48,96]{2,1,0:T(8,128)S(1)}, f32[1,48,96]{2,1,0:T(8,128)}, u32[]{:S(2)}) copy-start(f32[1,48,96]{2,1,0:T(8,128)} %param.11) | copy-start | bytes 55300
  22.2 40.6 %copy-start.3 = (f32[64]{0:T(128)S(1)}, f32[64]{0:T(128)}, u32[]{:S(2)}) copy-start(f32[64]{0:T(128)} %occ_ref.1) | copy-start | bytes 772
  36.0 22.4 %all-to-all-start = ((f32[16,40,128]{2,1,0:T(8,128)}), f32[16,40,128]{2,1,0:T(8,128)S(1)}, u32[]{:S(2)}, u32[]{:S(2)}) async-start(f32[16,40,128]{2,1,0:T(8,128)} %ladder.1), calls=%async_computation | async-start | bytes 655360 | tf_op jit(solution)/shard_map/all_to_all | solution.py:260
  46.8 11.7 %collective-permute-start = (f32[40,128]{1,0:T(8,128)S(1)}, f32[40,128]{1,0:T(8,128)S(1)}, u32[]{:S(2)}, u32[]{:S(2)}) collective-permute-start(f32[40,128]{1,0:T(8,128)S(1)} %get-tuple-element.12), channel_id=1, source_target_pairs={{0,128},{16,144},{32,160},{48,176},{64,192},{80,208},{96,224},{112... | collective-permute-start | bytes 61448 | tf_op jit(solution)/shard_map/ppermute | solution.py:273
  50.6 7.9 %collective-permute-start.1 = (f32[40,128]{1,0:T(8,128)S(1)}, f32[40,128]{1,0:T(8,128)S(1)}, u32[]{:S(2)}, u32[]{:S(2)}) collective-permute-start(f32[40,128]{1,0:T(8,128)S(1)} %get-tuple-element.13), channel_id=1, source_target_pairs={{0,256},{16,272},{32,288},{48,304},{64,320},{80,336},{96,352},{112... | collective-permute-start | bytes 61448 | tf_op jit(solution)/shard_map/ppermute | solution.py:273
  56.4 6.3 %collective-permute-start.2 = (f32[40,128]{1,0:T(8,128)S(1)}, f32[40,128]{1,0:T(8,128)S(1)}, u32[]{:S(2)}, u32[]{:S(2)}) collective-permute-start(f32[40,128]{1,0:T(8,128)S(1)} %get-tuple-element.14), channel_id=1, source_target_pairs={{0,384},{16,400},{32,416},{48,432},{64,448},{80,464},{96,480},{112... | collective-permute-start | bytes 61448 | tf_op jit(solution)/shard_map/ppermute | solution.py:273

commit v5 on v4

--- a/solution.py
+++ b/solution.py
@@ -10,7 +10,7 @@
 LANES = 128
 Y = 8
 SIZES = (2, 6, 8, 8, 8)
-CLASSES = 4
+NEAR = 2
 
 
 def split(x):
@@ -160,12 +160,12 @@
 def hole_kernel(occ_block, pair_ref, integral_ref, rows_ref, *out_refs):
     me = lax.axis_index("tile")
     my_z, my_y = lax.div(me, Y), lax.rem(me, Y)
-    low = lax.rem(my_z, CLASSES)
+    near = lax.div(my_z, NEAR) * NEAR
     count = rows_ref.shape[0]
-    sources = [(low + CLASSES * (i // Y)) * Y + i % Y for i in range(count)]
+    sources = [(near + i // Y) * Y + i % Y for i in range(count)]
     irreps = [irrep_of(pair_ref, source, occ_block) for source in sources]
     for step, out_ref in enumerate(out_refs):
-        target = lax.bitwise_xor(my_z, step) * Y + my_y
+        target = lax.bitwise_xor(my_z, NEAR * step) * Y + my_y
         irrep = irrep_of(pair_ref, target, occ_block)
         value = None
         for i in range(count):
@@ -208,10 +208,10 @@
     occ_block = occ_energy.shape[0] // 8
     vmem = pl.BlockSpec(memory_space=pltpu.VMEM)
     smem = pl.BlockSpec(memory_space=pltpu.SMEM)
-    spread = depth // CLASSES
+    classes = depth // NEAR
     groups = [
-        [(low + CLASSES * far) * Y + y for far in range(spread) for y in range(Y)]
-        for low in range(CLASSES)
+        [(far * NEAR + near) * Y + y for near in range(NEAR) for y in range(Y)]
+        for far in range(classes)
     ]
 
     hbm = pl.BlockSpec(memory_space=pltpu.MemorySpace.HBM)
@@ -222,7 +222,7 @@
 
     mine = pl.pallas_call(
         head_kernel,
-        out_shape=jax.ShapeDtypeStruct((spread * Y,) + packed, jnp.float32),
+        out_shape=jax.ShapeDtypeStruct((NEAR * Y,) + packed, jnp.float32),
         in_specs=[hbm],
         out_specs=vmem,
         scratch_shapes=[
@@ -261,20 +261,20 @@
     gathered, _ = lax.optimization_barrier((gathered, ladder))
     partial = pl.pallas_call(
         functools.partial(hole_kernel, occ_block),
-        out_shape=[jax.ShapeDtypeStruct(packed, jnp.float32)] * CLASSES,
+        out_shape=[jax.ShapeDtypeStruct(packed, jnp.float32)] * classes,
         in_specs=[smem, smem, vmem],
-        out_specs=[vmem] * CLASSES,
+        out_specs=[vmem] * classes,
         compiler_params=small,
         name="hole",
     )(pairs, hole_integrals, gathered)
     hole = [partial[0]]
-    for step in range(1, CLASSES):
-        route = [(z * Y + y, (z ^ step) * Y + y) for z in range(depth) for y in range(Y)]
+    for step in range(1, classes):
+        route = [(z * Y + y, (z ^ (NEAR * step)) * Y + y) for z in range(depth) for y in range(Y)]
         hole.append(lax.ppermute(partial[step], "tile", route))
     out = pl.pallas_call(
         functools.partial(final_kernel, occ_block),
         out_shape=jax.ShapeDtypeStruct((rows_dev, width), jnp.float32),
-        in_specs=[smem, smem] + [vmem] * (3 + CLASSES),
+        in_specs=[smem, smem] + [vmem] * (3 + classes),
         out_specs=vmem,
         compiler_params=small,
         name="final",

time: 65.2 us -> 62 us (0.951)
  the two profiles are of different devices: /device:TPU:1 before, /device:TPU:18 now
where the time goes in v5:
time: 62 us; the launch traced here: 61.5 us
  starting transfers between devices  39.6 us (64%)
  Pallas kernels  15.9 us (26%)
  waiting for transfers between devices  5.79 us (9%)
    ppermute x3, starting transfers between devices, local(): hole.append(lax.ppermute(partial[step], 'tile', route))  19.4 us
    pallas_call x1, Pallas kernels, local(): pl.pallas_call(functools.partial(ladder_kernel, occ_block, sizes), out_sh...  11.4 us
    all_to_all x1, starting transfers between devices, local(): lax.all_to_all(mine, 'tile', 0, 0, axis_index_groups=groups, tiled=True)  10.6 us
    all_to_all x1, starting transfers between devices, local(): pieces = lax.all_to_all(ladder, 'slab', 0, 0, tiled=True)  9.57 us
    ppermute x3, waiting for transfers between devices, local(): hole.append(lax.ppermute(partial[step], 'tile', route))  5.78 us
    pallas_call x1, Pallas kernels, local(): pl.pallas_call(head_kernel, out_shape=jax.ShapeDtypeStruct((NEAR * Y,) +...  1.81 us
    pallas_call x1, Pallas kernels, local(): pl.pallas_call(functools.partial(hole_kernel, occ_block), out_shape=[jax....  1.38 us
    pallas_call x1, Pallas kernels, local(): pl.pallas_call(functools.partial(final_kernel, occ_block), out_shape=jax....  1.26 us
  transfers between devices with their start and end apart: 5, of which 1 were waited for; matrix products, arithmetic and copies ran while one was open for 0% of the time, Pallas kernels for 21%

profile of v5, /device:TPU:18, one launch (start us, length us, event | category | flops | bytes accessed | tf_op | source)
XLA Modules:
  0.0 61.5 jit_solution(8296089670505991068)
XLA Ops:
  0.0 1.8 %head.1.after_ref = f32[16,40,128]{2,1,0:T(8,128)} custom-call(f32[96,768]{1,0:T(8,128)} %bitcast.11), custom_call_target="tpu_custom_call" | custom-call | tf_op jit(solution)/shard_map/head/pallas_call | solution.py:223
  1.8 10.6 %all-to-all-start.1 = ((f32[16,40,128]{2,1,0:T(8,128)}), f32[16,40,128]{2,1,0:T(8,128)S(1)}, u32[]{:S(2)}, u32[]{:S(2)}) async-start(f32[16,40,128]{2,1,0:T(8,128)} %head.1.after_ref), calls=%async_computation.1 | async-start | bytes 655360 | tf_op jit(solution)/shard_map/all_to_all | solution.py:236
  12.4 0.0 copy-start
  12.5 0.0 copy-start.2
  12.5 0.0 copy-start.4
  12.5 0.0 copy-start.1
  12.5 0.0 copy-start.3
  12.5 11.4 %ladder.1 = f32[16,40,128]{2,1,0:T(8,128)} custom-call(s32[2,64]{1,0:T(2,128)} %bitcast.8, f32[16,40,128]{2,1,0:T(8,128)} %head.1.after_ref, f32[96,768]{1,0:T(8,128)} %bitcast.12, f32[32,96,768]{2,1,0:T(8,128)} %bitcast.13), custom_call_target="tpu_custom_call" | custom-call | flops 6442450944 | bytes 9437184 | tf_op jit(solution)/shard_map/ladder/pallas_call | solution.py:240
  23.9 0.0 all-to-all-done.1.rows_ref
  23.9 9.6 %all-to-all-start = ((f32[16,40,128]{2,1,0:T(8,128)}), f32[16,40,128]{2,1,0:T(8,128)S(1)}, u32[]{:S(2)}, u32[]{:S(2)}) async-start(f32[16,40,128]{2,1,0:T(8,128)} %ladder.1), calls=%async_computation | async-start | bytes 655360 | tf_op jit(solution)/shard_map/all_to_all | solution.py:260
  33.5 0.0 copy-done
  33.5 0.0 copy-done.2
  33.5 1.4 %hole.1 = (f32[40,128]{1,0:T(8,128)S(1)}, f32[40,128]{1,0:T(8,128)S(1)}, f32[40,128]{1,0:T(8,128)S(1)}, f32[40,128]{1,0:T(8,128)S(1)}) custom-call(s32[2,64]{1,0:T(2,128)S(1)} %bitcast.9, f32[64,64]{1,0:T(8,128)S(1)} %copy-done, f32[16,40,128]{2,1,0:T(8,128)S(1)} %all-to-all-done.1.rows_ref), custom_call_target="tpu_custom_call" | custom-call | tf_op jit(solution)/shard_map/hole/pallas_call | solution.py:262
  34.9 5.7 %collective-permute-start = (f32[40,128]{1,0:T(8,128)S(1)}, f32[40,128]{1,0:T(8,128)S(1)}, u32[]{:S(2)}, u32[]{:S(2)}) collective-permute-start(f32[40,128]{1,0:T(8,128)S(1)} %get-tuple-element.12), channel_id=1, source_target_pairs={{0,256},{16,272},{32,288},{48,304},{64,320},{80,336},{96,352},{112... | collective-permute-start | bytes 61448 | tf_op jit(solution)/shard_map/ppermute | solution.py:273
  40.6 11.9 %collective-permute-start.1 = (f32[40,128]{1,0:T(8,128)S(1)}, f32[40,128]{1,0:T(8,128)S(1)}, u32[]{:S(2)}, u32[]{:S(2)}) collective-permute-start(f32[40,128]{1,0:T(8,128)S(1)} %get-tuple-element.13), channel_id=1, source_target_pairs={{0,512},{16,528},{32,544},{48,560},{64,576},{80,592},{96,608},{112... | collective-permute-start | bytes 61448 | tf_op jit(solution)/shard_map/ppermute | solution.py:273
  52.4 1.9 %collective-permute-start.2 = (f32[40,128]{1,0:T(8,128)S(1)}, f32[40,128]{1,0:T(8,128)S(1)}, u32[]{:S(2)}, u32[]{:S(2)}) collective-permute-start(f32[40,128]{1,0:T(8,128)S(1)} %get-tuple-element.14), channel_id=1, source_target_pairs={{0,768},{16,784},{32,800},{48,816},{64,832},{80,848},{96,864},{112... | collective-permute-start | bytes 61448 | tf_op jit(solution)/shard_map/ppermute | solution.py:273
  54.4 0.0 copy-done.4
  54.4 0.1 reshape.3.vir_ref
  54.4 0.0 all-to-all-done.ladder_ref
  54.4 0.0 collective-permute-done.refs_1_
  54.5 0.0 collective-permute-done.1.refs_2_
  54.5 5.8 %collective-permute-done.2.refs_3_ = f32[40,128]{1,0:T(8,128)S(1)} collective-permute-done((f32[40,128]{1,0:T(8,128)S(1)}, f32[40,128]{1,0:T(8,128)S(1)}, u32[]{:S(2)}, u32[]{:S(2)}) %collective-permute-start.2) | collective-permute-done | bytes 20512 | tf_op jit(solution)/shard_map/ppermute | solution.py:273
  60.2 0.0 copy-done.1
  60.2 0.0 copy-done.3
  60.2 1.3 %final.1 = f32[48,96]{1,0:T(8,128)} custom-call(s32[2,64]{1,0:T(2,128)S(1)} %bitcast.10, f32[64]{0:T(128)S(1)} %copy-done.3, f32[8,96]{1,0:T(8,128)S(1)} %reshape.3.vir_ref, f32[48,96]{1,0:T(8,128)S(1)} %bitcast.7, f32[16,40,128]{2,1,0:T(8,128)S(1)} %all-to-all-done.ladder_ref, f32[40,128]{1,0:T(8,128)S(1)} %get-tuple-element.11.refs_0_, ...), custom_call_target="tpu_custom_call" | custom-call | tf_op jit(solution)/shard_map/final/pallas_call | solution.py:274
Async XLA Ops:
  1.8 22.1 %all-to-all-start.1 = ((f32[16,40,128]{2,1,0:T(8,128)}), f32[16,40,128]{2,1,0:T(8,128)S(1)}, u32[]{:S(2)}, u32[]{:S(2)}) async-start(f32[16,40,128]{2,1,0:T(8,128)} %head.1.after_ref), calls=%async_computation.1 | async-start | bytes 655360 | tf_op jit(solution)/shard_map/all_to_all | solution.py:236
  12.4 21.1 %copy-start = (f32[64,64]{1,0:T(8,128)S(1)}, f32[64,64]{1,0:T(8,128)}, u32[]{:S(2)}) copy-start(f32[64,64]{1,0:T(8,128)} %integral_ref.1) | copy-start | bytes 49156
  12.5 21.1 %copy-start.2 = (s32[64,2]{0,1:T(2,128)S(1)}, s32[64,2]{0,1:T(2,128)}, u32[]{:S(2)}) copy-start(s32[64,2]{0,1:T(2,128)} %param.9) | copy-start | bytes 1540
  12.5 41.9 %copy-start.4 = (f32[768]{0:T(1024)S(1)}, f32[768]{0:T(1024)}, u32[]{:S(2)}) copy-start(f32[768]{0:T(1024)} %param.13) | copy-start | bytes 9220
  12.5 47.8 %copy-start.1 = (f32[1,48,96]{2,1,0:T(8,128)S(1)}, f32[1,48,96]{2,1,0:T(8,128)}, u32[]{:S(2)}) copy-start(f32[1,48,96]{2,1,0:T(8,128)} %param.11) | copy-start | bytes 55300
  12.5 47.8 %copy-start.3 = (f32[64]{0:T(128)S(1)}, f32[64]{0:T(128)}, u32[]{:S(2)}) copy-start(f32[64]{0:T(128)} %occ_ref.1) | copy-start | bytes 772
  23.9 30.5 %all-to-all-start = ((f32[16,40,128]{2,1,0:T(8,128)}), f32[16,40,128]{2,1,0:T(8,128)S(1)}, u32[]{:S(2)}, u32[]{:S(2)}) async-start(f32[16,40,128]{2,1,0:T(8,128)} %ladder.1), calls=%async_computation | async-start | bytes 655360 | tf_op jit(solution)/shard_map/all_to_all | solution.py:260
  34.9 19.5 %collective-permute-start = (f32[40,128]{1,0:T(8,128)S(1)}, f32[40,128]{1,0:T(8,128)S(1)}, u32[]{:S(2)}, u32[]{:S(2)}) collective-permute-start(f32[40,128]{1,0:T(8,128)S(1)} %get-tuple-element.12), channel_id=1, source_target_pairs={{0,256},{16,272},{32,288},{48,304},{64,320},{80,336},{96,352},{112... | collective-permute-start | bytes 61448 | tf_op jit(solution)/shard_map/ppermute | solution.py:273
  40.6 13.9 %collective-permute-start.1 = (f32[40,128]{1,0:T(8,128)S(1)}, f32[40,128]{1,0:T(8,128)S(1)}, u32[]{:S(2)}, u32[]{:S(2)}) collective-permute-start(f32[40,128]{1,0:T(8,128)S(1)} %get-tuple-element.13), channel_id=1, source_target_pairs={{0,512},{16,528},{32,544},{48,560},{64,576},{80,592},{96,608},{112... | collective-permute-start | bytes 61448 | tf_op jit(solution)/shard_map/ppermute | solution.py:273
  52.4 7.8 %collective-permute-start.2 = (f32[40,128]{1,0:T(8,128)S(1)}, f32[40,128]{1,0:T(8,128)S(1)}, u32[]{:S(2)}, u32[]{:S(2)}) collective-permute-start(f32[40,128]{1,0:T(8,128)S(1)} %get-tuple-element.14), channel_id=1, source_target_pairs={{0,768},{16,784},{32,800},{48,816},{64,832},{80,848},{96,864},{112... | collective-permute-start | bytes 61448 | tf_op jit(solution)/shard_map/ppermute | solution.py:273

commit v6 on v5

--- a/solution.py
+++ b/solution.py
@@ -268,7 +268,7 @@
         name="hole",
     )(pairs, hole_integrals, gathered)
     hole = [partial[0]]
-    for step in range(1, classes):
+    for step in sorted(range(1, classes), key=lambda step: min(step, classes - step)):
         route = [(z * Y + y, (z ^ (NEAR * step)) * Y + y) for z in range(depth) for y in range(Y)]
         hole.append(lax.ppermute(partial[step], "tile", route))
     out = pl.pallas_call(

time: 62 us -> 61.6 us (level)
  the two profiles are of different devices: /device:TPU:18 before, /device:TPU:1 now
where the time goes in v6:
time: 61.6 us; the launch traced here: 60.6 us
  starting transfers between devices  39.8 us (65%)
  Pallas kernels  15.9 us (26%)
  waiting for transfers between devices  4.66 us (8%)
    ppermute x3, starting transfers between devices, local(): hole.append(lax.ppermute(partial[step], 'tile', route))  18.8 us
    pallas_call x1, Pallas kernels, local(): pl.pallas_call(functools.partial(ladder_kernel, occ_block, sizes), out_sh...  11.4 us
    all_to_all x1, starting transfers between devices, local(): lax.all_to_all(mine, 'tile', 0, 0, axis_index_groups=groups, tiled=True)  10.9 us
    all_to_all x1, starting transfers between devices, local(): pieces = lax.all_to_all(ladder, 'slab', 0, 0, tiled=True)  10.1 us
    ppermute x3, waiting for transfers between devices, local(): hole.append(lax.ppermute(partial[step], 'tile', route))  4.66 us
    pallas_call x1, Pallas kernels, local(): pl.pallas_call(head_kernel, out_shape=jax.ShapeDtypeStruct((NEAR * Y,) +...  1.8 us
    pallas_call x1, Pallas kernels, local(): pl.pallas_call(functools.partial(hole_kernel, occ_block), out_shape=[jax....  1.38 us
    pallas_call x1, Pallas kernels, local(): pl.pallas_call(functools.partial(final_kernel, occ_block), out_shape=jax....  1.26 us
  transfers between devices with their start and end apart: 5, of which 1 were waited for; matrix products, arithmetic and copies ran while one was open for 0% of the time, Pallas kernels for 21%

profile of v6, /device:TPU:1, one launch (start us, length us, event | category | flops | bytes accessed | tf_op | source)
XLA Modules:
  0.0 60.6 jit_solution(6964599449495521647)
XLA Ops:
  0.0 1.8 %head.1.after_ref = f32[16,40,128]{2,1,0:T(8,128)} custom-call(f32[96,768]{1,0:T(8,128)} %bitcast.11), custom_call_target="tpu_custom_call" | custom-call | tf_op jit(solution)/shard_map/head/pallas_call | solution.py:223
  1.8 10.9 %all-to-all-start.1 = ((f32[16,40,128]{2,1,0:T(8,128)}), f32[16,40,128]{2,1,0:T(8,128)S(1)}, u32[]{:S(2)}, u32[]{:S(2)}) async-start(f32[16,40,128]{2,1,0:T(8,128)} %head.1.after_ref), calls=%async_computation.1 | async-start | bytes 655360 | tf_op jit(solution)/shard_map/all_to_all | solution.py:236
  12.8 0.0 copy-start
  12.8 0.0 copy-start.2
  12.8 0.0 copy-start.4
  12.8 0.0 copy-start.1
  12.8 0.0 copy-start.3
  12.8 11.4 %ladder.1 = f32[16,40,128]{2,1,0:T(8,128)} custom-call(s32[2,64]{1,0:T(2,128)} %bitcast.8, f32[16,40,128]{2,1,0:T(8,128)} %head.1.after_ref, f32[96,768]{1,0:T(8,128)} %bitcast.12, f32[32,96,768]{2,1,0:T(8,128)} %bitcast.13), custom_call_target="tpu_custom_call" | custom-call | flops 6442450944 | bytes 9437184 | tf_op jit(solution)/shard_map/ladder/pallas_call | solution.py:240
  24.2 0.0 all-to-all-done.1.rows_ref
  24.2 10.1 %all-to-all-start = ((f32[16,40,128]{2,1,0:T(8,128)}), f32[16,40,128]{2,1,0:T(8,128)S(1)}, u32[]{:S(2)}, u32[]{:S(2)}) async-start(f32[16,40,128]{2,1,0:T(8,128)} %ladder.1), calls=%async_computation | async-start | bytes 655360 | tf_op jit(solution)/shard_map/all_to_all | solution.py:260
  34.4 0.0 copy-done
  34.4 0.0 copy-done.2
  34.4 1.4 %hole.1 = (f32[40,128]{1,0:T(8,128)S(1)}, f32[40,128]{1,0:T(8,128)S(1)}, f32[40,128]{1,0:T(8,128)S(1)}, f32[40,128]{1,0:T(8,128)S(1)}) custom-call(s32[2,64]{1,0:T(2,128)S(1)} %bitcast.9, f32[64,64]{1,0:T(8,128)S(1)} %copy-done, f32[16,40,128]{2,1,0:T(8,128)S(1)} %all-to-all-done.1.rows_ref), custom_call_target="tpu_custom_call" | custom-call | tf_op jit(solution)/shard_map/hole/pallas_call | solution.py:262
  35.8 5.3 %collective-permute-start = (f32[40,128]{1,0:T(8,128)S(1)}, f32[40,128]{1,0:T(8,128)S(1)}, u32[]{:S(2)}, u32[]{:S(2)}) collective-permute-start(f32[40,128]{1,0:T(8,128)S(1)} %get-tuple-element.12), channel_id=1, source_target_pairs={{0,256},{16,272},{32,288},{48,304},{64,320},{80,336},{96,352},{112... | collective-permute-start | bytes 61448 | tf_op jit(solution)/shard_map/ppermute | solution.py:273
  41.0 9.5 %collective-permute-start.1 = (f32[40,128]{1,0:T(8,128)S(1)}, f32[40,128]{1,0:T(8,128)S(1)}, u32[]{:S(2)}, u32[]{:S(2)}) collective-permute-start(f32[40,128]{1,0:T(8,128)S(1)} %get-tuple-element.13), channel_id=1, source_target_pairs={{0,768},{16,784},{32,800},{48,816},{64,832},{80,848},{96,864},{112... | collective-permute-start | bytes 61448 | tf_op jit(solution)/shard_map/ppermute | solution.py:273
  50.6 4.0 %collective-permute-start.2 = (f32[40,128]{1,0:T(8,128)S(1)}, f32[40,128]{1,0:T(8,128)S(1)}, u32[]{:S(2)}, u32[]{:S(2)}) collective-permute-start(f32[40,128]{1,0:T(8,128)S(1)} %get-tuple-element.14), channel_id=1, source_target_pairs={{0,512},{16,528},{32,544},{48,560},{64,576},{80,592},{96,608},{112... | collective-permute-start | bytes 61448 | tf_op jit(solution)/shard_map/ppermute | solution.py:273
  54.6 0.0 copy-done.4
  54.6 0.1 reshape.3.vir_ref
  54.6 0.0 all-to-all-done.ladder_ref
  54.6 0.0 collective-permute-done.refs_1_
  54.7 0.0 collective-permute-done.1.refs_2_
  54.7 4.7 %collective-permute-done.2.refs_3_ = f32[40,128]{1,0:T(8,128)S(1)} collective-permute-done((f32[40,128]{1,0:T(8,128)S(1)}, f32[40,128]{1,0:T(8,128)S(1)}, u32[]{:S(2)}, u32[]{:S(2)}) %collective-permute-start.2) | collective-permute-done | bytes 20512 | tf_op jit(solution)/shard_map/ppermute | solution.py:273
  59.3 0.0 copy-done.1
  59.3 0.0 copy-done.3
  59.3 1.3 %final.1 = f32[48,96]{1,0:T(8,128)} custom-call(s32[2,64]{1,0:T(2,128)S(1)} %bitcast.10, f32[64]{0:T(128)S(1)} %copy-done.3, f32[8,96]{1,0:T(8,128)S(1)} %reshape.3.vir_ref, f32[48,96]{1,0:T(8,128)S(1)} %bitcast.7, f32[16,40,128]{2,1,0:T(8,128)S(1)} %all-to-all-done.ladder_ref, f32[40,128]{1,0:T(8,128)S(1)} %get-tuple-element.11.refs_0_, ...), custom_call_target="tpu_custom_call" | custom-call | tf_op jit(solution)/shard_map/final/pallas_call | solution.py:274
Async XLA Ops:
  1.8 22.4 %all-to-all-start.1 = ((f32[16,40,128]{2,1,0:T(8,128)}), f32[16,40,128]{2,1,0:T(8,128)S(1)}, u32[]{:S(2)}, u32[]{:S(2)}) async-start(f32[16,40,128]{2,1,0:T(8,128)} %head.1.after_ref), calls=%async_computation.1 | async-start | bytes 655360 | tf_op jit(solution)/shard_map/all_to_all | solution.py:236
  12.8 21.6 %copy-start = (f32[64,64]{1,0:T(8,128)S(1)}, f32[64,64]{1,0:T(8,128)}, u32[]{:S(2)}) copy-start(f32[64,64]{1,0:T(8,128)} %integral_ref.1) | copy-start | bytes 49156
  12.8 21.6 %copy-start.2 = (s32[64,2]{0,1:T(2,128)S(1)}, s32[64,2]{0,1:T(2,128)}, u32[]{:S(2)}) copy-start(s32[64,2]{0,1:T(2,128)} %param.9) | copy-start | bytes 1540
  12.8 41.8 %copy-start.4 = (f32[768]{0:T(1024)S(1)}, f32[768]{0:T(1024)}, u32[]{:S(2)}) copy-start(f32[768]{0:T(1024)} %param.13) | copy-start | bytes 9220
  12.8 46.5 %copy-start.1 = (f32[1,48,96]{2,1,0:T(8,128)S(1)}, f32[1,48,96]{2,1,0:T(8,128)}, u32[]{:S(2)}) copy-start(f32[1,48,96]{2,1,0:T(8,128)} %param.11) | copy-start | bytes 55300
  12.8 46.5 %copy-start.3 = (f32[64]{0:T(128)S(1)}, f32[64]{0:T(128)}, u32[]{:S(2)}) copy-start(f32[64]{0:T(128)} %occ_ref.1) | copy-start | bytes 772
  24.2 30.4 %all-to-all-start = ((f32[16,40,128]{2,1,0:T(8,128)}), f32[16,40,128]{2,1,0:T(8,128)S(1)}, u32[]{:S(2)}, u32[]{:S(2)}) async-start(f32[16,40,128]{2,1,0:T(8,128)} %ladder.1), calls=%async_computation | async-start | bytes 655360 | tf_op jit(solution)/shard_map/all_to_all | solution.py:260
  35.8 18.9 %collective-permute-start = (f32[40,128]{1,0:T(8,128)S(1)}, f32[40,128]{1,0:T(8,128)S(1)}, u32[]{:S(2)}, u32[]{:S(2)}) collective-permute-start(f32[40,128]{1,0:T(8,128)S(1)} %get-tuple-element.12), channel_id=1, source_target_pairs={{0,256},{16,272},{32,288},{48,304},{64,320},{80,336},{96,352},{112... | collective-permute-start | bytes 61448 | tf_op jit(solution)/shard_map/ppermute | solution.py:273
  41.0 13.6 %collective-permute-start.1 = (f32[40,128]{1,0:T(8,128)S(1)}, f32[40,128]{1,0:T(8,128)S(1)}, u32[]{:S(2)}, u32[]{:S(2)}) collective-permute-start(f32[40,128]{1,0:T(8,128)S(1)} %get-tuple-element.13), channel_id=1, source_target_pairs={{0,768},{16,784},{32,800},{48,816},{64,832},{80,848},{96,864},{112... | collective-permute-start | bytes 61448 | tf_op jit(solution)/shard_map/ppermute | solution.py:273
  50.6 8.8 %collective-permute-start.2 = (f32[40,128]{1,0:T(8,128)S(1)}, f32[40,128]{1,0:T(8,128)S(1)}, u32[]{:S(2)}, u32[]{:S(2)}) collective-permute-start(f32[40,128]{1,0:T(8,128)S(1)} %get-tuple-element.14), channel_id=1, source_target_pairs={{0,512},{16,528},{32,544},{48,560},{64,576},{80,592},{96,608},{112... | collective-permute-start | bytes 61448 | tf_op jit(solution)/shard_map/ppermute | solution.py:273

commit v7 on v6

--- a/solution.py
+++ b/solution.py
@@ -63,8 +63,8 @@
 
 
 def ladder_kernel(
-    occ_block, sizes, pair_ref, after_ref, amp_hbm, vec_hbm, out_ref,
-    weight, left_even, left_odd, amp_t, vectors, total, sem,
+    occ_block, sizes, pair_ref, after_ref, amp_hbm, vec_hbm, out_hbm,
+    weight, left_even, left_odd, amp_t, vectors, total, out_ref, sem, out_sem,
 ):
     _, width, rows_all = vectors.shape
     lefts = (left_even, left_odd)
@@ -121,6 +121,22 @@
             middle, other, (((1,), (1,)), ((), ())), preferred_element_type=jnp.float32
         )
         total[block] = value if c == 0 else total[block] + value
+
+    def store(block):
+        part = pl.ds(2 * block, 2)
+        return pltpu.make_async_copy(out_ref.at[part], out_hbm.at[part], out_sem.at[block])
+
+    def finish(block):
+        half = width // 2
+        value = (
+            total[block, :width, :width]
+            + total[block, :width, width:]
+            + total[block, width:, :width]
+            + total[block, width:, width:]
+        )
+        for part in range(2):
+            pack(out_ref.at[2 * block + part], value[part * half : (part + 1) * half])
+        store(block).start()
 
     load_amp.wait()
     amp = jnp.transpose(amp_t[...])
@@ -144,17 +160,10 @@
         following = first(*work[index + 1]) if index + 1 < len(work) else None
         second(c, block, middle)
         middle = following
-    half = width // 2
+        if c + 1 == len(sizes):
+            finish(block)
     for block in range(8):
-        value = (
-            total[block, :width, :width]
-            + total[block, :width, width:]
-            + total[block, width:, :width]
-            + total[block, width:, width:]
-        )
-        for part in range(2):
-            piece = 2 * block + part
-            pack(out_ref.at[piece], value[part * half : (part + 1) * half])
+        store(block).wait()
 
 
 def hole_kernel(occ_block, pair_ref, integral_ref, rows_ref, *out_refs):
@@ -241,7 +250,7 @@
         functools.partial(ladder_kernel, occ_block, sizes),
         out_shape=jax.ShapeDtypeStruct((slabs,) + packed, jnp.float32),
         in_specs=[smem, hbm, hbm, hbm],
-        out_specs=vmem,
+        out_specs=hbm,
         scratch_shapes=[
             pltpu.VMEM((8, 2 * LANES, 2 * LANES), jnp.bfloat16),
             pltpu.VMEM((max(sizes[::2]), rows_all, 2 * LANES), jnp.bfloat16),
@@ -249,7 +258,9 @@
             pltpu.VMEM((width, rows_all), jnp.float32),
             pltpu.VMEM((vectors, width, rows_all), jnp.float32),
             pltpu.VMEM((8, 2 * width, 2 * width), jnp.float32),
+            pltpu.VMEM((slabs,) + packed, jnp.float32),
             pltpu.SemaphoreType.DMA((sizes[0] + len(sizes),)),
+            pltpu.SemaphoreType.DMA((8,)),
         ],
         compiler_params=pltpu.CompilerParams(vmem_limit_bytes=58 << 20),
         cost_estimate=pl.CostEstimate(

time: 61.6 us -> 61.6 us (level)
  no operation moved by 1% of the time
where the time goes in v7:
time: 61.6 us; the launch traced here: 60.5 us
  starting transfers between devices  39.8 us (65%)
  Pallas kernels  15.8 us (26%)
  waiting for transfers between devices  4.66 us (8%)
    ppermute x3, starting transfers between devices, local(): hole.append(lax.ppermute(partial[step], 'tile', route))  18.8 us
    pallas_call x1, Pallas kernels, local(): pl.pallas_call(functools.partial(ladder_kernel, occ_block, sizes), out_sh...  11.4 us
    all_to_all x1, starting transfers between devices, local(): lax.all_to_all(mine, 'tile', 0, 0, axis_index_groups=groups, tiled=True)  10.9 us
    all_to_all x1, starting transfers between devices, local(): pieces = lax.all_to_all(ladder, 'slab', 0, 0, tiled=True)  10.1 us
    ppermute x3, waiting for transfers between devices, local(): hole.append(lax.ppermute(partial[step], 'tile', route))  4.66 us
    pallas_call x1, Pallas kernels, local(): pl.pallas_call(head_kernel, out_shape=jax.ShapeDtypeStruct((NEAR * Y,) +...  1.8 us
    pallas_call x1, Pallas kernels, local(): pl.pallas_call(functools.partial(hole_kernel, occ_block), out_shape=[jax....  1.38 us
    pallas_call x1, Pallas kernels, local(): pl.pallas_call(functools.partial(final_kernel, occ_block), out_shape=jax....  1.26 us
  transfers between devices with their start and end apart: 5, of which 1 were waited for; matrix products, arithmetic and copies ran while one was open for 0% of the time, Pallas kernels for 21%

profile of v7, /device:TPU:1, one launch (start us, length us, event | category | flops | bytes accessed | tf_op | source)
XLA Modules:
  0.0 60.5 jit_solution(15325316989249005953)
XLA Ops:
  0.0 1.8 %head.1.after_ref = f32[16,40,128]{2,1,0:T(8,128)} custom-call(f32[96,768]{1,0:T(8,128)} %bitcast.11), custom_call_target="tpu_custom_call" | custom-call | tf_op jit(solution)/shard_map/head/pallas_call | solution.py:232
  1.8 10.9 %all-to-all-start.1 = ((f32[16,40,128]{2,1,0:T(8,128)}), f32[16,40,128]{2,1,0:T(8,128)S(1)}, u32[]{:S(2)}, u32[]{:S(2)}) async-start(f32[16,40,128]{2,1,0:T(8,128)} %head.1.after_ref), calls=%async_computation.1 | async-start | bytes 655360 | tf_op jit(solution)/shard_map/all_to_all | solution.py:245
  12.8 0.0 copy-start
  12.8 0.0 copy-start.2
  12.8 0.0 copy-start.4
  12.8 0.0 copy-start.1
  12.8 0.0 copy-start.3
  12.8 11.4 %ladder.1 = f32[16,40,128]{2,1,0:T(8,128)} custom-call(s32[2,64]{1,0:T(2,128)} %bitcast.8, f32[16,40,128]{2,1,0:T(8,128)} %head.1.after_ref, f32[96,768]{1,0:T(8,128)} %bitcast.12, f32[32,96,768]{2,1,0:T(8,128)} %bitcast.13), custom_call_target="tpu_custom_call" | custom-call | flops 6442450944 | bytes 9437184 | tf_op jit(solution)/shard_map/ladder/pallas_call | solution.py:249
  24.2 0.0 all-to-all-done.1.rows_ref
  24.2 10.1 %all-to-all-start = ((f32[16,40,128]{2,1,0:T(8,128)}), f32[16,40,128]{2,1,0:T(8,128)S(1)}, u32[]{:S(2)}, u32[]{:S(2)}) async-start(f32[16,40,128]{2,1,0:T(8,128)} %ladder.1), calls=%async_computation | async-start | bytes 655360 | tf_op jit(solution)/shard_map/all_to_all | solution.py:271
  34.3 0.0 copy-done
  34.3 0.0 copy-done.2
  34.3 1.4 %hole.1 = (f32[40,128]{1,0:T(8,128)S(1)}, f32[40,128]{1,0:T(8,128)S(1)}, f32[40,128]{1,0:T(8,128)S(1)}, f32[40,128]{1,0:T(8,128)S(1)}) custom-call(s32[2,64]{1,0:T(2,128)S(1)} %bitcast.9, f32[64,64]{1,0:T(8,128)S(1)} %copy-done, f32[16,40,128]{2,1,0:T(8,128)S(1)} %all-to-all-done.1.rows_ref), custom_call_target="tpu_custom_call" | custom-call | tf_op jit(solution)/shard_map/hole/pallas_call | solution.py:273
  35.7 5.3 %collective-permute-start = (f32[40,128]{1,0:T(8,128)S(1)}, f32[40,128]{1,0:T(8,128)S(1)}, u32[]{:S(2)}, u32[]{:S(2)}) collective-permute-start(f32[40,128]{1,0:T(8,128)S(1)} %get-tuple-element.12), channel_id=1, source_target_pairs={{0,256},{16,272},{32,288},{48,304},{64,320},{80,336},{96,352},{112... | collective-permute-start | bytes 61448 | tf_op jit(solution)/shard_map/ppermute | solution.py:284
  41.0 9.5 %collective-permute-start.1 = (f32[40,128]{1,0:T(8,128)S(1)}, f32[40,128]{1,0:T(8,128)S(1)}, u32[]{:S(2)}, u32[]{:S(2)}) collective-permute-start(f32[40,128]{1,0:T(8,128)S(1)} %get-tuple-element.13), channel_id=1, source_target_pairs={{0,768},{16,784},{32,800},{48,816},{64,832},{80,848},{96,864},{112... | collective-permute-start | bytes 61448 | tf_op jit(solution)/shard_map/ppermute | solution.py:284
  50.5 4.0 %collective-permute-start.2 = (f32[40,128]{1,0:T(8,128)S(1)}, f32[40,128]{1,0:T(8,128)S(1)}, u32[]{:S(2)}, u32[]{:S(2)}) collective-permute-start(f32[40,128]{1,0:T(8,128)S(1)} %get-tuple-element.14), channel_id=1, source_target_pairs={{0,512},{16,528},{32,544},{48,560},{64,576},{80,592},{96,608},{112... | collective-permute-start | bytes 61448 | tf_op jit(solution)/shard_map/ppermute | solution.py:284
  54.5 0.0 copy-done.4
  54.5 0.1 reshape.3.vir_ref
  54.6 0.0 all-to-all-done.ladder_ref
  54.6 0.0 collective-permute-done.refs_1_
  54.6 0.0 collective-permute-done.1.refs_2_
  54.6 4.7 %collective-permute-done.2.refs_3_ = f32[40,128]{1,0:T(8,128)S(1)} collective-permute-done((f32[40,128]{1,0:T(8,128)S(1)}, f32[40,128]{1,0:T(8,128)S(1)}, u32[]{:S(2)}, u32[]{:S(2)}) %collective-permute-start.2) | collective-permute-done | bytes 20512 | tf_op jit(solution)/shard_map/ppermute | solution.py:284
  59.3 0.0 copy-done.1
  59.3 0.0 copy-done.3
  59.3 1.3 %final.1 = f32[48,96]{1,0:T(8,128)} custom-call(s32[2,64]{1,0:T(2,128)S(1)} %bitcast.10, f32[64]{0:T(128)S(1)} %copy-done.3, f32[8,96]{1,0:T(8,128)S(1)} %reshape.3.vir_ref, f32[48,96]{1,0:T(8,128)S(1)} %bitcast.7, f32[16,40,128]{2,1,0:T(8,128)S(1)} %all-to-all-done.ladder_ref, f32[40,128]{1,0:T(8,128)S(1)} %get-tuple-element.11.refs_0_, ...), custom_call_target="tpu_custom_call" | custom-call | tf_op jit(solution)/shard_map/final/pallas_call | solution.py:285
Async XLA Ops:
  1.8 22.4 %all-to-all-start.1 = ((f32[16,40,128]{2,1,0:T(8,128)}), f32[16,40,128]{2,1,0:T(8,128)S(1)}, u32[]{:S(2)}, u32[]{:S(2)}) async-start(f32[16,40,128]{2,1,0:T(8,128)} %head.1.after_ref), calls=%async_computation.1 | async-start | bytes 655360 | tf_op jit(solution)/shard_map/all_to_all | solution.py:245
  12.8 21.5 %copy-start = (f32[64,64]{1,0:T(8,128)S(1)}, f32[64,64]{1,0:T(8,128)}, u32[]{:S(2)}) copy-start(f32[64,64]{1,0:T(8,128)} %integral_ref.1) | copy-start | bytes 49156
  12.8 21.5 %copy-start.2 = (s32[64,2]{0,1:T(2,128)S(1)}, s32[64,2]{0,1:T(2,128)}, u32[]{:S(2)}) copy-start(s32[64,2]{0,1:T(2,128)} %param.9) | copy-start | bytes 1540
  12.8 41.7 %copy-start.4 = (f32[768]{0:T(1024)S(1)}, f32[768]{0:T(1024)}, u32[]{:S(2)}) copy-start(f32[768]{0:T(1024)} %param.13) | copy-start | bytes 9220
  12.8 46.5 %copy-start.1 = (f32[1,48,96]{2,1,0:T(8,128)S(1)}, f32[1,48,96]{2,1,0:T(8,128)}, u32[]{:S(2)}) copy-start(f32[1,48,96]{2,1,0:T(8,128)} %param.11) | copy-start | bytes 55300
  12.8 46.5 %copy-start.3 = (f32[64]{0:T(128)S(1)}, f32[64]{0:T(128)}, u32[]{:S(2)}) copy-start(f32[64]{0:T(128)} %occ_ref.1) | copy-start | bytes 772
  24.2 30.4 %all-to-all-start = ((f32[16,40,128]{2,1,0:T(8,128)}), f32[16,40,128]{2,1,0:T(8,128)S(1)}, u32[]{:S(2)}, u32[]{:S(2)}) async-start(f32[16,40,128]{2,1,0:T(8,128)} %ladder.1), calls=%async_computation | async-start | bytes 655360 | tf_op jit(solution)/shard_map/all_to_all | solution.py:271
  35.7 18.9 %collective-permute-start = (f32[40,128]{1,0:T(8,128)S(1)}, f32[40,128]{1,0:T(8,128)S(1)}, u32[]{:S(2)}, u32[]{:S(2)}) collective-permute-start(f32[40,128]{1,0:T(8,128)S(1)} %get-tuple-element.12), channel_id=1, source_target_pairs={{0,256},{16,272},{32,288},{48,304},{64,320},{80,336},{96,352},{112... | collective-permute-start | bytes 61448 | tf_op jit(solution)/shard_map/ppermute | solution.py:284
  41.0 13.6 %collective-permute-start.1 = (f32[40,128]{1,0:T(8,128)S(1)}, f32[40,128]{1,0:T(8,128)S(1)}, u32[]{:S(2)}, u32[]{:S(2)}) collective-permute-start(f32[40,128]{1,0:T(8,128)S(1)} %get-tuple-element.13), channel_id=1, source_target_pairs={{0,768},{16,784},{32,800},{48,816},{64,832},{80,848},{96,864},{112... | collective-permute-start | bytes 61448 | tf_op jit(solution)/shard_map/ppermute | solution.py:284
  50.5 8.8 %collective-permute-start.2 = (f32[40,128]{1,0:T(8,128)S(1)}, f32[40,128]{1,0:T(8,128)S(1)}, u32[]{:S(2)}, u32[]{:S(2)}) collective-permute-start(f32[40,128]{1,0:T(8,128)S(1)} %get-tuple-element.14), channel_id=1, source_target_pairs={{0,512},{16,528},{32,544},{48,560},{64,576},{80,592},{96,608},{112... | collective-permute-start | bytes 61448 | tf_op jit(solution)/shard_map/ppermute | solution.py:284

commit v8 on v6

--- a/solution.py
+++ b/solution.py
@@ -72,14 +72,13 @@
     irrep = irrep_of(pair_ref, lax.axis_index("tile"), occ_block)
     pieces = [(q, 1) for q in range(sizes[0])] + list(zip(starts[1:], sizes[1:]))
     load_amp = pltpu.make_async_copy(amp_hbm, amp_t, sem.at[len(pieces)])
-    load_amp.start()
     loads = [
         pltpu.make_async_copy(
             vec_hbm.at[pl.ds(begin, size)], vectors.at[pl.ds(begin, size)], sem.at[index]
         )
         for index, (begin, size) in enumerate(pieces)
     ]
-    for load in loads:
+    for load in loads[: sizes[0]] + [load_amp] + loads[sizes[0] :]:
         load.start()
     weight[...] = jnp.zeros_like(weight)
     fill = jnp.zeros((LANES - width, rows_all), jnp.bfloat16)
@@ -122,6 +121,9 @@
         )
         total[block] = value if c == 0 else total[block] + value
 
+    for q in range(sizes[0]):
+        loads[q].wait()
+        prepare(0, q)
     load_amp.wait()
     amp = jnp.transpose(amp_t[...])
     for block in range(8):
@@ -129,9 +131,6 @@
         for row in (0, LANES):
             weight[block, row : row + width, :width] = high
             weight[block, row : row + width, LANES : LANES + width] = low
-    for q in range(sizes[0]):
-        loads[q].wait()
-        prepare(0, q)
     work = [(c, block) for c in range(len(sizes)) for block in range(8)]
     middle = first(*work[0])
     for index, (c, block) in enumerate(work):

time: 61.6 us -> 61.6 us (level)
  no operation moved by 1% of the time
where the time goes in v8:
time: 61.6 us; the launch traced here: 60.6 us
  starting transfers between devices  39.8 us (65%)
  Pallas kernels  15.9 us (26%)
  waiting for transfers between devices  4.66 us (8%)
    ppermute x3, starting transfers between devices, local(): hole.append(lax.ppermute(partial[step], 'tile', route))  18.8 us
    pallas_call x1, Pallas kernels, local(): pl.pallas_call(functools.partial(ladder_kernel, occ_block, sizes), out_sh...  11.4 us
    all_to_all x1, starting transfers between devices, local(): lax.all_to_all(mine, 'tile', 0, 0, axis_index_groups=groups, tiled=True)  10.9 us
    all_to_all x1, starting transfers between devices, local(): pieces = lax.all_to_all(ladder, 'slab', 0, 0, tiled=True)  10.1 us
    ppermute x3, waiting for transfers between devices, local(): hole.append(lax.ppermute(partial[step], 'tile', route))  4.66 us
    pallas_call x1, Pallas kernels, local(): pl.pallas_call(head_kernel, out_shape=jax.ShapeDtypeStruct((NEAR * Y,) +...  1.8 us
    pallas_call x1, Pallas kernels, local(): pl.pallas_call(functools.partial(hole_kernel, occ_block), out_shape=[jax....  1.38 us
    pallas_call x1, Pallas kernels, local(): pl.pallas_call(functools.partial(final_kernel, occ_block), out_shape=jax....  1.26 us
  transfers between devices with their start and end apart: 5, of which 1 were waited for; matrix products, arithmetic and copies ran while one was open for 0% of the time, Pallas kernels for 21%

profile of v8, /device:TPU:1, one launch (start us, length us, event | category | flops | bytes accessed | tf_op | source)
XLA Modules:
  0.0 60.6 jit_solution(13749588091631833460)
XLA Ops:
  0.0 1.8 %head.1.after_ref = f32[16,40,128]{2,1,0:T(8,128)} custom-call(f32[96,768]{1,0:T(8,128)} %bitcast.11), custom_call_target="tpu_custom_call" | custom-call | tf_op jit(solution)/shard_map/head/pallas_call | solution.py:222
  1.8 10.9 %all-to-all-start.1 = ((f32[16,40,128]{2,1,0:T(8,128)}), f32[16,40,128]{2,1,0:T(8,128)S(1)}, u32[]{:S(2)}, u32[]{:S(2)}) async-start(f32[16,40,128]{2,1,0:T(8,128)} %head.1.after_ref), calls=%async_computation.1 | async-start | bytes 655360 | tf_op jit(solution)/shard_map/all_to_all | solution.py:235
  12.8 0.0 copy-start
  12.8 0.0 copy-start.2
  12.8 0.0 copy-start.4
  12.8 0.0 copy-start.1
  12.8 0.0 copy-start.3
  12.8 11.4 %ladder.1 = f32[16,40,128]{2,1,0:T(8,128)} custom-call(s32[2,64]{1,0:T(2,128)} %bitcast.8, f32[16,40,128]{2,1,0:T(8,128)} %head.1.after_ref, f32[96,768]{1,0:T(8,128)} %bitcast.12, f32[32,96,768]{2,1,0:T(8,128)} %bitcast.13), custom_call_target="tpu_custom_call" | custom-call | flops 6442450944 | bytes 9437184 | tf_op jit(solution)/shard_map/ladder/pallas_call | solution.py:239
  24.2 0.0 all-to-all-done.1.rows_ref
  24.2 10.1 %all-to-all-start = ((f32[16,40,128]{2,1,0:T(8,128)}), f32[16,40,128]{2,1,0:T(8,128)S(1)}, u32[]{:S(2)}, u32[]{:S(2)}) async-start(f32[16,40,128]{2,1,0:T(8,128)} %ladder.1), calls=%async_computation | async-start | bytes 655360 | tf_op jit(solution)/shard_map/all_to_all | solution.py:259
  34.4 0.0 copy-done
  34.4 0.0 copy-done.2
  34.4 1.4 %hole.1 = (f32[40,128]{1,0:T(8,128)S(1)}, f32[40,128]{1,0:T(8,128)S(1)}, f32[40,128]{1,0:T(8,128)S(1)}, f32[40,128]{1,0:T(8,128)S(1)}) custom-call(s32[2,64]{1,0:T(2,128)S(1)} %bitcast.9, f32[64,64]{1,0:T(8,128)S(1)} %copy-done, f32[16,40,128]{2,1,0:T(8,128)S(1)} %all-to-all-done.1.rows_ref), custom_call_target="tpu_custom_call" | custom-call | tf_op jit(solution)/shard_map/hole/pallas_call | solution.py:261
  35.8 5.3 %collective-permute-start = (f32[40,128]{1,0:T(8,128)S(1)}, f32[40,128]{1,0:T(8,128)S(1)}, u32[]{:S(2)}, u32[]{:S(2)}) collective-permute-start(f32[40,128]{1,0:T(8,128)S(1)} %get-tuple-element.12), channel_id=1, source_target_pairs={{0,256},{16,272},{32,288},{48,304},{64,320},{80,336},{96,352},{112... | collective-permute-start | bytes 61448 | tf_op jit(solution)/shard_map/ppermute | solution.py:272
  41.1 9.5 %collective-permute-start.1 = (f32[40,128]{1,0:T(8,128)S(1)}, f32[40,128]{1,0:T(8,128)S(1)}, u32[]{:S(2)}, u32[]{:S(2)}) collective-permute-start(f32[40,128]{1,0:T(8,128)S(1)} %get-tuple-element.13), channel_id=1, source_target_pairs={{0,768},{16,784},{32,800},{48,816},{64,832},{80,848},{96,864},{112... | collective-permute-start | bytes 61448 | tf_op jit(solution)/shard_map/ppermute | solution.py:272
  50.6 4.0 %collective-permute-start.2 = (f32[40,128]{1,0:T(8,128)S(1)}, f32[40,128]{1,0:T(8,128)S(1)}, u32[]{:S(2)}, u32[]{:S(2)}) collective-permute-start(f32[40,128]{1,0:T(8,128)S(1)} %get-tuple-element.14), channel_id=1, source_target_pairs={{0,512},{16,528},{32,544},{48,560},{64,576},{80,592},{96,608},{112... | collective-permute-start | bytes 61448 | tf_op jit(solution)/shard_map/ppermute | solution.py:272
  54.6 0.0 copy-done.4
  54.6 0.1 reshape.3.vir_ref
  54.6 0.0 all-to-all-done.ladder_ref
  54.7 0.0 collective-permute-done.refs_1_
  54.7 0.0 collective-permute-done.1.refs_2_
  54.7 4.7 %collective-permute-done.2.refs_3_ = f32[40,128]{1,0:T(8,128)S(1)} collective-permute-done((f32[40,128]{1,0:T(8,128)S(1)}, f32[40,128]{1,0:T(8,128)S(1)}, u32[]{:S(2)}, u32[]{:S(2)}) %collective-permute-start.2) | collective-permute-done | bytes 20512 | tf_op jit(solution)/shard_map/ppermute | solution.py:272
  59.3 0.0 copy-done.1
  59.3 0.0 copy-done.3
  59.3 1.3 %final.1 = f32[48,96]{1,0:T(8,128)} custom-call(s32[2,64]{1,0:T(2,128)S(1)} %bitcast.10, f32[64]{0:T(128)S(1)} %copy-done.3, f32[8,96]{1,0:T(8,128)S(1)} %reshape.3.vir_ref, f32[48,96]{1,0:T(8,128)S(1)} %bitcast.7, f32[16,40,128]{2,1,0:T(8,128)S(1)} %all-to-all-done.ladder_ref, f32[40,128]{1,0:T(8,128)S(1)} %get-tuple-element.11.refs_0_, ...), custom_call_target="tpu_custom_call" | custom-call | tf_op jit(solution)/shard_map/final/pallas_call | solution.py:273
Async XLA Ops:
  1.8 22.4 %all-to-all-start.1 = ((f32[16,40,128]{2,1,0:T(8,128)}), f32[16,40,128]{2,1,0:T(8,128)S(1)}, u32[]{:S(2)}, u32[]{:S(2)}) async-start(f32[16,40,128]{2,1,0:T(8,128)} %head.1.after_ref), calls=%async_computation.1 | async-start | bytes 655360 | tf_op jit(solution)/shard_map/all_to_all | solution.py:235
  12.8 21.6 %copy-start = (f32[64,64]{1,0:T(8,128)S(1)}, f32[64,64]{1,0:T(8,128)}, u32[]{:S(2)}) copy-start(f32[64,64]{1,0:T(8,128)} %integral_ref.1) | copy-start | bytes 49156
  12.8 21.6 %copy-start.2 = (s32[64,2]{0,1:T(2,128)S(1)}, s32[64,2]{0,1:T(2,128)}, u32[]{:S(2)}) copy-start(s32[64,2]{0,1:T(2,128)} %param.9) | copy-start | bytes 1540
  12.8 41.8 %copy-start.4 = (f32[768]{0:T(1024)S(1)}, f32[768]{0:T(1024)}, u32[]{:S(2)}) copy-start(f32[768]{0:T(1024)} %param.13) | copy-start | bytes 9220
  12.8 46.5 %copy-start.1 = (f32[1,48,96]{2,1,0:T(8,128)S(1)}, f32[1,48,96]{2,1,0:T(8,128)}, u32[]{:S(2)}) copy-start(f32[1,48,96]{2,1,0:T(8,128)} %param.11) | copy-start | bytes 55300
  12.8 46.5 %copy-start.3 = (f32[64]{0:T(128)S(1)}, f32[64]{0:T(128)}, u32[]{:S(2)}) copy-start(f32[64]{0:T(128)} %occ_ref.1) | copy-start | bytes 772
  24.2 30.4 %all-to-all-start = ((f32[16,40,128]{2,1,0:T(8,128)}), f32[16,40,128]{2,1,0:T(8,128)S(1)}, u32[]{:S(2)}, u32[]{:S(2)}) async-start(f32[16,40,128]{2,1,0:T(8,128)} %ladder.1), calls=%async_computation | async-start | bytes 655360 | tf_op jit(solution)/shard_map/all_to_all | solution.py:259
  35.8 18.9 %collective-permute-start = (f32[40,128]{1,0:T(8,128)S(1)}, f32[40,128]{1,0:T(8,128)S(1)}, u32[]{:S(2)}, u32[]{:S(2)}) collective-permute-start(f32[40,128]{1,0:T(8,128)S(1)} %get-tuple-element.12), channel_id=1, source_target_pairs={{0,256},{16,272},{32,288},{48,304},{64,320},{80,336},{96,352},{112... | collective-permute-start | bytes 61448 | tf_op jit(solution)/shard_map/ppermute | solution.py:272
  41.1 13.6 %collective-permute-start.1 = (f32[40,128]{1,0:T(8,128)S(1)}, f32[40,128]{1,0:T(8,128)S(1)}, u32[]{:S(2)}, u32[]{:S(2)}) collective-permute-start(f32[40,128]{1,0:T(8,128)S(1)} %get-tuple-element.13), channel_id=1, source_target_pairs={{0,768},{16,784},{32,800},{48,816},{64,832},{80,848},{96,864},{112... | collective-permute-start | bytes 61448 | tf_op jit(solution)/shard_map/ppermute | solution.py:272
  50.6 8.8 %collective-permute-start.2 = (f32[40,128]{1,0:T(8,128)S(1)}, f32[40,128]{1,0:T(8,128)S(1)}, u32[]{:S(2)}, u32[]{:S(2)}) collective-permute-start(f32[40,128]{1,0:T(8,128)S(1)} %get-tuple-element.14), channel_id=1, source_target_pairs={{0,512},{16,528},{32,544},{48,560},{64,576},{80,592},{96,608},{112... | collective-permute-start | bytes 61448 | tf_op jit(solution)/shard_map/ppermute | solution.py:272
